TPU v7x, 128 devices: a whole 4x4x4 slice. The times are simulated.
128 devices in a mesh: patch: 32 (over y, z, core), band: 4 (over x).
Axes of the slice: x: 4, y: 4, z: 4, core: 2. Of those that a mesh axis runs over, the one named last changes fastest.
Arguments:
- blocks: bfloat16 [4, 1024, 256, 256], P('band', 'patch'), may hold values from -6 to 6
- dest_patch: int32 [4, 1024], P('band', 'patch'), may hold values from 0 to 31, as said below
- dest_slot: int32 [4, 1024], P('band', 'patch'), may hold values from 0 to 3
- weights: bfloat16 [4, 1024], P('band', 'patch'), may hold values from 0.25 to 4
- psf_taps: bfloat16 [4, 1024, 2, 41], P('band', 'patch'), may hold values from -1 to 1
- det_taps: float32 [4, 25], P('band'), may hold values from -1.25 to 1.25
- noise_var: float32 [4], P('band'), may hold values from 0.5 to 2
Outputs:
- coadd_image: float32 [4, 512, 16384], P('band', None, 'patch')
- chi_square: float32 [512, 16384], P('band', 'patch')
Inputs may be any that keep to these rules, and one draw needn't show every extreme that they name: `dest_patch`: within each band, among the 32 blocks of one index of patch (aligned runs of 32 blocks), at most 4 go to any one patch; in every band some patch receives exactly 4 blocks from every index of patch.
All inputs are finite; a program needn't handle non-finite values.
Results may differ from a plain program's by a relative error of at most 0.0048.
Values may be sent and summed in bfloat16 or wider, within the bound.
A program may use at most 192 MiB of HBM per device.

v0:
```python
import math

import jax
import jax.numpy as jnp
from jax import lax
from jax.sharding import PartitionSpec as P

TH = 2
TW = 2
DR = 12
CAP = 4
SLOTS = 4


def padded_2(shard, sides, width):
    for axis, dim in sides:
        size, length = (lax.axis_size(axis), shard.shape[dim])
        up = [(i, (i + 1) % size) for i in range(size)]
        down = [(j, i) for i, j in up]
        last = lax.slice_in_dim(shard, length - width, length, axis=dim)
        initial = lax.slice_in_dim(shard, 0, width, axis=dim)
        before = lax.ppermute(last, axis, up)
        after = lax.ppermute(initial, axis, down)
        shard = jnp.concatenate([before, shard, after], axis=dim)
    return shard


def offset_grid(rows, cols, start):
    row_index = lax.broadcasted_iota(jnp.int32, (rows, cols), 0)
    col_index = lax.broadcasted_iota(jnp.int32, (rows, cols), 1)
    return col_index - row_index + start


def tap_onehot(tap_count, number, start):
    offsets = offset_grid(number, number, start)
    return (offsets[None, :, :] == jnp.arange(tap_count, dtype=jnp.int32)[:, None, None]).astype(
        jnp.bfloat16
    )


def banded_float(kernel, rows, cols, start):
    offsets = offset_grid(rows, cols, start)
    table = jnp.zeros((rows, cols), jnp.float32)
    for tap_index in range(kernel.shape[0]):
        table = table + jnp.where(
            offsets == tap_index, kernel[tap_index], jnp.zeros((), jnp.float32)
        )
    return table


def match_blocks(raw_blocks, block_taps):
    number = raw_blocks.shape[0]
    block_edge = raw_blocks.shape[-1]
    tap_count = block_taps.shape[-1]
    groups = math.gcd(number, 8)
    per_group = number // groups
    onehot = tap_onehot(tap_count, block_edge, tap_count // 2)

    def match_group(grouped):
        group_blocks, group_taps = grouped
        matrices = jnp.einsum(
            "nct,tij->ncij", group_taps, onehot, preferred_element_type=jnp.float32
        ).astype(jnp.bfloat16)
        half_pass = jnp.einsum(
            "nij,njk->nik", matrices[:, 0], group_blocks, preferred_element_type=jnp.float32
        ).astype(jnp.bfloat16)
        return jnp.einsum(
            "nij,nkj->nik", half_pass, matrices[:, 1], preferred_element_type=jnp.float32
        ).astype(jnp.bfloat16)

    matched = lax.map(
        match_group,
        (
            raw_blocks.reshape(groups, per_group, block_edge, block_edge),
            block_taps.reshape(groups, per_group, 2, tap_count),
        ),
    )
    return matched.reshape(number, block_edge, block_edge)


def local(blocks, dest_patch, dest_slot, weights, psf_taps, det_taps, noise_var):
    npatch = lax.axis_size("patch")
    local_blocks = blocks[0]
    block_edge = local_blocks.shape[-1]
    tap_count = psf_taps.shape[-1]
    target = dest_patch[0]
    dest_hits = (target[:, None] == jnp.arange(npatch, dtype=jnp.int32)[None, :]).astype(jnp.int32)
    earlier = jnp.cumsum(dest_hits, axis=0) - dest_hits
    slot_rank = jnp.sum(earlier * dest_hits, axis=1)
    position = target * CAP + slot_rank
    total_slots = npatch * CAP
    weight_buffer = (
        jnp.zeros((total_slots,), jnp.bfloat16).at[position].set(weights[0]).reshape(npatch, CAP)
    )
    tile_buffer = (
        jnp.zeros((total_slots,), jnp.int32).at[position].set(dest_slot[0]).reshape(npatch, CAP)
    )
    block_buffer = (
        jnp.zeros((total_slots, block_edge, block_edge), jnp.bfloat16)
        .at[position]
        .set(local_blocks)
    )
    block_buffer = block_buffer.reshape(npatch, CAP, block_edge, block_edge)
    taps_buffer = jnp.zeros((total_slots, 2, tap_count), jnp.bfloat16).at[position].set(psf_taps[0])
    taps_buffer = taps_buffer.reshape(npatch, CAP, 2, tap_count)
    raw_blocks = lax.all_to_all(block_buffer, "patch", split_axis=0, concat_axis=0, tiled=True)
    block_taps = lax.all_to_all(taps_buffer, "patch", split_axis=0, concat_axis=0, tiled=True)
    arrived_weights = lax.all_to_all(
        weight_buffer, "patch", split_axis=0, concat_axis=0, tiled=True
    )
    arrived_tiles = lax.all_to_all(tile_buffer, "patch", split_axis=0, concat_axis=0, tiled=True)
    sources = raw_blocks.shape[0]
    items = raw_blocks.shape[1]
    matched_here = match_blocks(
        raw_blocks.reshape(sources * items, block_edge, block_edge),
        block_taps.reshape(sources * items, 2, tap_count),
    )
    received = matched_here.reshape(sources, items, block_edge, block_edge)
    arrived_blocks = received.reshape(total_slots, block_edge, block_edge)
    tile_picks = (
        arrived_tiles.reshape(1, total_slots) == jnp.arange(SLOTS, dtype=jnp.int32)[:, None]
    )
    selected = jnp.where(
        tile_picks, arrived_weights.reshape(1, total_slots), jnp.zeros((), jnp.bfloat16)
    )
    weighted = lax.dot_general(
        selected, arrived_blocks, (((1,), (0,)), ((), ())), preferred_element_type=jnp.float32
    )
    weight_sum = jnp.sum(selected.astype(jnp.float32), axis=1)
    tile_values = weighted / jnp.maximum(weight_sum, 1.0)[:, None, None]
    tile_rows = []
    for row_index in range(TH):
        tile_rows.append(
            jnp.concatenate(
                [tile_values[row_index * TW + col_index] for col_index in range(TW)], axis=1
            )
        )
    patch_image = jnp.concatenate(tile_rows, axis=0)
    kernel = det_taps[0]
    padded = padded_2(patch_image, (("patch", 1),), DR)
    columns = patch_image.shape[1]
    pixel_rows = patch_image.shape[0]
    col_table = banded_float(kernel, columns, columns + 2 * DR, 0)
    col_pass = lax.dot_general(
        padded, col_table, (((1,), (1,)), ((), ())), precision=lax.Precision.HIGHEST
    )
    row_table = banded_float(kernel, pixel_rows, pixel_rows, DR)
    row_pass = jnp.dot(row_table, col_pass, precision=lax.Precision.HIGHEST)
    band_term = row_pass * row_pass / noise_var[0]
    chi_part = lax.psum_scatter(band_term, "band", scatter_dimension=0, tiled=True)
    return (patch_image[None], chi_part)


def solution(mesh):
    in_specs = (
        P("band", "patch", None, None),
        P("band", "patch"),
        P("band", "patch"),
        P("band", "patch"),
        P("band", "patch", None, None),
        P("band", None),
        P("band"),
    )
    out_specs = (P("band", None, "patch"), P("band", "patch"))
    return jax.shard_map(local, mesh=mesh, in_specs=in_specs, out_specs=out_specs, check_vma=False)
```

profile of v0, /device:TPU:0, one launch (start us, length us, event | category | flops | bytes accessed | tf_op | source)
XLA Modules:
  0.0 496.0 jit_solution(16414624245147336647)
XLA Ops:
  7.2 0.7 fusion.353
  7.9 0.8 select_reduce_fusion
  8.8 0.7 fusion.358
  9.5 0.9 scatter_custom_fusion.1
  10.3 0.7 all_to_all.24
  11.1 8.4 %all-to-all-start.1 = ((bf16[32,1,4]{2,1,0:T(2,128)(2,1)}), bf16[32,1,4]{2,1,0:T(2,128)(2,1)S(1)}, u32[]{:S(2)}, u32[]{:S(2)}) async-start(bf16[32,1,4]{2,1,0:T(2,128)(2,1)} %all_to_all.24), calls=%async_computation.1 | async-start | bytes 32768 | tf_op jit(solution)/shard_map/all_to_all | solution.py:108
  19.5 0.8 scatter_custom_fusion
  20.3 0.7 all_to_all.18
  21.0 5.8 %all-to-all-done.1 = bf16[32,1,4]{2,1,0:T(2,128)(2,1)S(1)} async-done(((bf16[32,1,4]{2,1,0:T(2,128)(2,1)}), bf16[32,1,4]{2,1,0:T(2,128)(2,1)S(1)}, u32[]{:S(2)}, u32[]{:S(2)}) %all-to-all-start.1) | async-done | bytes 288 | tf_op jit(solution)/shard_map/all_to_all | solution.py:108
  26.8 3.8 all-to-all-start
  30.7 2.8 scatter_fusion
  33.6 0.7 reshape.165
  34.3 3.6 all-to-all-done
  37.9 3.9 all-to-all-start.2
  41.8 5.9 %broadcast_in_dim.260 = bf16[128,256,256]{2,1,0:T(8,128)(2,1)} broadcast(bf16[]{:T(256)} %constant.38.clone.1), dimensions={} | broadcast | bytes 16777218 | tf_op jit(solution)/shard_map/broadcast_in_dim | solution.py:99
  47.7 11.3 %scatter_fusion.1 = bf16[128,256,256]{2,1,0:T(8,128)(2,1)} fusion(bf16[128,256,256]{2,1,0:T(8,128)(2,1)} %broadcast_in_dim.260, s32[32]{0:T(128)S(1)} %fusion.358, bf16[32,256,256]{2,1,0:T(8,128)(2,1)} %bitcast.104), kind=kCustom, calls=%fused_computation.3 | custom fusion | bytes 12583040 | tf_op jit(solution)/shard_map/scatter | solution.py:101
  59.0 7.8 %all-to-all-start.3 = ((bf16[32,4,256,256]{3,2,1,0:T(8,128)(2,1)}), bf16[32,4,256,256]{3,2,1,0:T(8,128)(2,1)}, u32[]{:S(2)}, u32[]{:S(2)}) async-start(bf16[32,4,256,256]{3,2,1,0:T(8,128)(2,1)} %bitcast.102), calls=%async_computation.3 | async-start | bytes 33554432 | tf_op jit(solution)/shard_map/all_to_all | solution.py:106
  66.9 0.7 fusion.421
  67.6 0.1 reduce.1
  67.7 0.1 broadcast_in_dim.255
  67.8 0.5 broadcast.63
  68.3 0.7 reduce.4
  69.0 0.1 eq.344
  69.1 0.1 convert_reduce_fusion
  69.2 0.1 reshape.166
  69.4 238.3 %all-to-all-done.3 = bf16[32,4,256,256]{3,2,1,0:T(8,128)(2,1)} async-done(((bf16[32,4,256,256]{3,2,1,0:T(8,128)(2,1)}), bf16[32,4,256,256]{3,2,1,0:T(8,128)(2,1)}, u32[]{:S(2)}, u32[]{:S(2)}) %all-to-all-start.3) | async-done | bytes 16777248 | tf_op jit(solution)/shard_map/all_to_all | solution.py:106
  307.7 66.4 %while.11 = (s32[]{:T(128)}, bf16[8,16,256,256]{3,2,1,0:T(8,128)(2,1)}, bf16[8,16,2,41]{3,1,0,2:T(8,128)(2,1)S(1)}, bf16[8,16,256,256]{3,2,1,0:T(8,128)(2,1)}, s32[256,256]{1,0:T(8,128)S(1)}, /*index=5*/s32[]{:T(128)}) while((s32[]{:T(128)}, bf16[8,16,256,256]{3,2,1,0:T(8,128)(2,1)}, bf16[8,16,2,41]{3,1,0,2:T(8,128)(2,1)S(1)}, ...), condition=%wide.region_7.8_spmd.clone, body=%wide.region_6.7_spmd.clone.sunk | while | flops 1255276544 | bytes 21242952 | solution.py:71
  307.7 1.2 fusion.437
  309.0 1.6 slice_bitcast_fusion.7
  310.5 5.5 %bitcast_dynamic-update-slice_fusion.2 = bf16[8,16,256,256]{3,2,1,0:T(8,128)(2,1)} fusion(bf16[8,16,256,256]{3,2,1,0:T(8,128)(2,1)} %get-tuple-element.150, s32[]{:T(128)} %get-tuple-element.149, bf16[16,256,256]{2,0,1:T(8,128)(2,1)} %get-tuple-element.141, bf16[8,16,256,256]{3,2,1,0:T(8,128)(2,1)} %get-tuple-element.158, ...), kind=kOutput, calls=%fused_computation.13.clone.1 | convolution fusion | flops 1075838976 | bytes 8389632 | tf_op jit(solution)/shard_map/while/body/eval_jaxpr/nij,nkj->nik/dot_general | solution.py:67
  316.0 1.2 fusion.437
  317.3 1.6 slice_bitcast_fusion.7
  318.9 5.4 %bitcast_dynamic-update-slice_fusion.2 = bf16[8,16,256,256]{3,2,1,0:T(8,128)(2,1)} fusion(bf16[8,16,256,256]{3,2,1,0:T(8,128)(2,1)} %get-tuple-element.150, s32[]{:T(128)} %get-tuple-element.149, bf16[16,256,256]{2,0,1:T(8,128)(2,1)} %get-tuple-element.141, bf16[8,16,256,256]{3,2,1,0:T(8,128)(2,1)} %get-tuple-element.158, ...), kind=kOutput, calls=%fused_computation.13.clone.1 | convolution fusion | flops 1075838976 | bytes 8389632 | tf_op jit(solution)/shard_map/while/body/eval_jaxpr/nij,nkj->nik/dot_general | solution.py:67
  324.3 1.2 fusion.437
  325.5 1.6 slice_bitcast_fusion.7
  327.1 5.5 %bitcast_dynamic-update-slice_fusion.2 = bf16[8,16,256,256]{3,2,1,0:T(8,128)(2,1)} fusion(bf16[8,16,256,256]{3,2,1,0:T(8,128)(2,1)} %get-tuple-element.150, s32[]{:T(128)} %get-tuple-element.149, bf16[16,256,256]{2,0,1:T(8,128)(2,1)} %get-tuple-element.141, bf16[8,16,256,256]{3,2,1,0:T(8,128)(2,1)} %get-tuple-element.158, ...), kind=kOutput, calls=%fused_computation.13.clone.1 | convolution fusion | flops 1075838976 | bytes 8389632 | tf_op jit(solution)/shard_map/while/body/eval_jaxpr/nij,nkj->nik/dot_general | solution.py:67
  332.6 1.2 fusion.437
  333.8 1.6 slice_bitcast_fusion.7
  335.4 5.5 %bitcast_dynamic-update-slice_fusion.2 = bf16[8,16,256,256]{3,2,1,0:T(8,128)(2,1)} fusion(bf16[8,16,256,256]{3,2,1,0:T(8,128)(2,1)} %get-tuple-element.150, s32[]{:T(128)} %get-tuple-element.149, bf16[16,256,256]{2,0,1:T(8,128)(2,1)} %get-tuple-element.141, bf16[8,16,256,256]{3,2,1,0:T(8,128)(2,1)} %get-tuple-element.158, ...), kind=kOutput, calls=%fused_computation.13.clone.1 | convolution fusion | flops 1075838976 | bytes 8389632 | tf_op jit(solution)/shard_map/while/body/eval_jaxpr/nij,nkj->nik/dot_general | solution.py:67
  340.9 1.2 fusion.437
  342.1 1.6 slice_bitcast_fusion.7
  343.7 5.5 %bitcast_dynamic-update-slice_fusion.2 = bf16[8,16,256,256]{3,2,1,0:T(8,128)(2,1)} fusion(bf16[8,16,256,256]{3,2,1,0:T(8,128)(2,1)} %get-tuple-element.150, s32[]{:T(128)} %get-tuple-element.149, bf16[16,256,256]{2,0,1:T(8,128)(2,1)} %get-tuple-element.141, bf16[8,16,256,256]{3,2,1,0:T(8,128)(2,1)} %get-tuple-element.158, ...), kind=kOutput, calls=%fused_computation.13.clone.1 | convolution fusion | flops 1075838976 | bytes 8389632 | tf_op jit(solution)/shard_map/while/body/eval_jaxpr/nij,nkj->nik/dot_general | solution.py:67
  349.3 1.2 fusion.437
  350.5 1.6 slice_bitcast_fusion.7
  352.1 5.4 %bitcast_dynamic-update-slice_fusion.2 = bf16[8,16,256,256]{3,2,1,0:T(8,128)(2,1)} fusion(bf16[8,16,256,256]{3,2,1,0:T(8,128)(2,1)} %get-tuple-element.150, s32[]{:T(128)} %get-tuple-element.149, bf16[16,256,256]{2,0,1:T(8,128)(2,1)} %get-tuple-element.141, bf16[8,16,256,256]{3,2,1,0:T(8,128)(2,1)} %get-tuple-element.158, ...), kind=kOutput, calls=%fused_computation.13.clone.1 | convolution fusion | flops 1075838976 | bytes 8389632 | tf_op jit(solution)/shard_map/while/body/eval_jaxpr/nij,nkj->nik/dot_general | solution.py:67
  357.5 1.2 fusion.437
  358.8 1.6 slice_bitcast_fusion.7
  360.4 5.5 %bitcast_dynamic-update-slice_fusion.2 = bf16[8,16,256,256]{3,2,1,0:T(8,128)(2,1)} fusion(bf16[8,16,256,256]{3,2,1,0:T(8,128)(2,1)} %get-tuple-element.150, s32[]{:T(128)} %get-tuple-element.149, bf16[16,256,256]{2,0,1:T(8,128)(2,1)} %get-tuple-element.141, bf16[8,16,256,256]{3,2,1,0:T(8,128)(2,1)} %get-tuple-element.158, ...), kind=kOutput, calls=%fused_computation.13.clone.1 | convolution fusion | flops 1075838976 | bytes 8389632 | tf_op jit(solution)/shard_map/while/body/eval_jaxpr/nij,nkj->nik/dot_general | solution.py:67
  365.9 1.2 fusion.437
  367.1 1.6 slice_bitcast_fusion.7
  368.7 5.5 %bitcast_dynamic-update-slice_fusion.2 = bf16[8,16,256,256]{3,2,1,0:T(8,128)(2,1)} fusion(bf16[8,16,256,256]{3,2,1,0:T(8,128)(2,1)} %get-tuple-element.150, s32[]{:T(128)} %get-tuple-element.149, bf16[16,256,256]{2,0,1:T(8,128)(2,1)} %get-tuple-element.141, bf16[8,16,256,256]{3,2,1,0:T(8,128)(2,1)} %get-tuple-element.158, ...), kind=kOutput, calls=%fused_computation.13.clone.1 | convolution fusion | flops 1075838976 | bytes 8389632 | tf_op jit(solution)/shard_map/while/body/eval_jaxpr/nij,nkj->nik/dot_general | solution.py:67
  374.2 14.7 %fusion.38 = f32[4,256,256]{2,0,1:T(4,128)S(1)} fusion(bf16[128,256,256]{2,1,0:T(8,128)(2,1)} %bitcast.103, s32[128]{0:T(128)S(1)} %eq.344, bf16[128]{0:T(256)(128)(2,1)S(1)} %broadcast_in_dim.255), kind=kOutput, calls=%fused_computation.25 | convolution fusion | flops 67109888 | bytes 17826560 | tf_op jit(solution)/shard_map/dot_general | solution.py:126
  388.8 0.3 copy_divide_fusion
  389.1 0.1 slice_bitcast_fusion.5
  389.2 1.1 maximum_maximum_fusion
  390.3 0.1 fusion.420
  390.4 0.1 collective-permute-start
  390.5 5.1 %collective-permute-start.1 = (f32[512,12]{1,0:T(8,128)S(1)}, f32[512,12]{1,0:T(8,128)S(1)}, u32[]{:S(2)}, u32[]{:S(2)}) collective-permute-start(f32[512,12]{1,0:T(8,128)S(1)} %get-tuple-element.76), channel_id=1, source_target_pairs={{4,0},{8,4},{12,8},{16,12},{20,16},{24,20},{28,24},{32,28},{36,32}... | collective-permute-start | bytes 73736 | tf_op jit(solution)/shard_map/ppermute | solution.py:23
  395.6 0.7 fusion.422
  396.9 2.7 collective-permute-done
  399.6 21.5 %collective-permute-done.1 = f32[512,12]{1,0:T(8,128)S(1)} collective-permute-done((f32[512,12]{1,0:T(8,128)S(1)}, f32[512,12]{1,0:T(8,128)S(1)}, u32[]{:S(2)}, u32[]{:S(2)}) %collective-permute-start.1) | collective-permute-done | bytes 24608 | tf_op jit(solution)/shard_map/ppermute | solution.py:23
  421.2 18.7 %fusion.41 = f32[512,512]{1,0:T(8,128)S(1)} fusion(f32[512,12]{1,0:T(8,128)S(1)} %collective-permute-done.1, f32[256,256]{1,0:T(8,128)S(1)} %get-tuple-element.80, f32[256,256]{1,0:T(8,128)S(1)} %get-tuple-element.81, f32[256,256]{1,0:T(8,128)S(1)} %get-tuple-element.82, f32[256,256]{1,0:T(8,128)S(1)} %get-tuple-element.79, ...), kind=kOutput, calls=%fused_computation.29 | convolution fusion | flops 1708064768 | bytes 2146404 | tf_op jit(solution)/shard_map/dot_general | solution.py:144
  439.9 21.6 %fusion.40 = f32[512,512]{1,0:T(8,128)} fusion(f32[512,512]{1,0:T(8,128)S(1)} %fusion.41, f32[]{:T(128)} %bitcast.101, f32[]{:T(128)} %bitcast.44, f32[]{:T(128)} %bitcast.43, f32[]{:T(128)} %bitcast.42, f32[]{:T(128)} %bitcast.41, f32[]{:T(128)} %bitcast.40, f32[]{:T(128)} %bitcast.39, f32[]{:T(128)} %bitcast.38, f32[]{:T(128)} %bitcast.37, f32[]{:T(128)} %bitcast.36, ...), kind=kOutput, calls=%fused_computation.28 | convolution fusion | flops 1631059968 | bytes 2097256 | tf_op jit(solution)/shard_map/dot_general | solution.py:148
  461.5 27.7 %reduce-scatter.2.cloned.1.call-done = f32[128,512]{1,0:T(8,128)} async-done(((f32[512,512]{1,0:T(8,128)}), f32[128,512]{1,0:T(8,128)}) %reduce-scatter.2.cloned.1.call-update) | async-done | bytes 262160 | tf_op jit(solution)/shard_map/reduce_scatter | solution.py:150
  (12 shorter events, 0.2 us)
Async XLA Ops:
  11.1 15.7 %all-to-all-start.1 = ((bf16[32,1,4]{2,1,0:T(2,128)(2,1)}), bf16[32,1,4]{2,1,0:T(2,128)(2,1)S(1)}, u32[]{:S(2)}, u32[]{:S(2)}) async-start(bf16[32,1,4]{2,1,0:T(2,128)(2,1)} %all_to_all.24), calls=%async_computation.1 | async-start | bytes 32768 | tf_op jit(solution)/shard_map/all_to_all | solution.py:108
  26.8 11.1 %all-to-all-start = ((s32[32,1,4]{2,1,0:T(1,128)}), s32[32,1,4]{2,1,0:T(1,128)S(1)}, u32[]{:S(2)}, u32[]{:S(2)}) async-start(s32[32,1,4]{2,1,0:T(1,128)} %bitcast.5), calls=%async_computation | async-start | bytes 32768 | tf_op jit(solution)/shard_map/all_to_all | solution.py:111
  37.9 21.1 %all-to-all-start.2 = ((bf16[32,2,164]{2,1,0:T(2,128)(2,1)}), bf16[32,2,164]{2,1,0:T(2,128)(2,1)S(1)}, u32[]{:S(2)}, u32[]{:S(2)}) async-start(bf16[32,2,164]{2,1,0:T(2,128)(2,1)} %reshape.165), calls=%async_computation.2 | async-start | bytes 65536 | tf_op jit(solution)/shard_map/all_to_all | solution.py:107
  59.0 7.9 %copy-start = (f32[1,25]{1,0:T(1,128)S(1)}, f32[1,25]{1,0:T(1,128)}, u32[]{:S(2)}) copy-start(f32[1,25]{1,0:T(1,128)} %param.14) | copy-start | bytes 304
  59.0 248.7 %all-to-all-start.3 = ((bf16[32,4,256,256]{3,2,1,0:T(8,128)(2,1)}), bf16[32,4,256,256]{3,2,1,0:T(8,128)(2,1)}, u32[]{:S(2)}, u32[]{:S(2)}) async-start(bf16[32,4,256,256]{3,2,1,0:T(8,128)(2,1)} %bitcast.102), calls=%async_computation.3 | async-start | bytes 33554432 | tf_op jit(solution)/shard_map/all_to_all | solution.py:106
  66.8 422.3 %reduce-scatter.2.cloned.1.call-start = ((), (), s32[]{:S(2)}) async-start(), calls=%async_computation.5 | async-start | bytes 1310720 | tf_op jit(solution)/shard_map/reduce_scatter | solution.py:150
  390.4 9.2 %collective-permute-start = (f32[512,12]{1,0:T(8,128)S(1)}, f32[512,12]{1,0:T(8,128)S(1)}, u32[]{:S(2)}, u32[]{:S(2)}) collective-permute-start(f32[512,12]{1,0:T(8,128)S(1)} %get-tuple-element.75), channel_id=1, source_target_pairs={{0,4},{4,8},{8,12},{12,16},{16,20},{20,24},{24,28},{28,32},{32,36}... | collective-permute-start | bytes 73736 | tf_op jit(solution)/shard_map/ppermute | solution.py:22
  390.5 30.6 %collective-permute-start.1 = (f32[512,12]{1,0:T(8,128)S(1)}, f32[512,12]{1,0:T(8,128)S(1)}, u32[]{:S(2)}, u32[]{:S(2)}) collective-permute-start(f32[512,12]{1,0:T(8,128)S(1)} %get-tuple-element.76), channel_id=1, source_target_pairs={{4,0},{8,4},{12,8},{16,12},{20,16},{24,20},{28,24},{32,28},{36,32}... | collective-permute-start | bytes 73736 | tf_op jit(solution)/shard_map/ppermute | solution.py:23
Sparse Core Ops, SparseCore 0:
  461.6 27.4 reduce-scatter.1
where the time goes:
time: 497 us; the launch traced here: 496 us
  waiting for transfers between devices  300 us (60%)
  matrix products  109 us (22%)
  local copies, waits for them, and re-layouts  39.1 us (8%)
  starting transfers between devices  29.1 us (6%)
  between operations  14.8 us (3%)
    all_to_all x1, waiting for transfers between devices, local(): lax.all_to_all(block_buffer, 'patch', split_axis=0, concat_axis=0, tiled=...  238 us
    dot_general x8, matrix products, match_group(): jnp.einsum('nij,nkj->nik', half_pass, matrices[:, 1], preferred_element_t...  43.8 us
    reduce_scatter x1, waiting for transfers between devices, local(): lax.psum_scatter(band_term, 'band', scatter_dimension=0, tiled=True)  27.7 us
    dot_general x1, matrix products, local(): row_pass = jnp.dot(row_table, col_pass, precision=lax.Precision.HIGHEST)  21.6 us
    ppermute x1, waiting for transfers between devices, padded_2(): after = lax.ppermute(initial, axis, down)  21.5 us
    dot_general x1, matrix products, local(): lax.dot_general(padded, col_table, (((1,), (1,)), ((), ())), precision=la...  18.7 us
    dot_general x1, matrix products, local(): lax.dot_general(selected, arrived_blocks, (((1,), (0,)), ((), ())), prefe...  14.7 us
    squeeze x8, local copies, waits for them, and re-layouts, match_group(): matrices[:, 0]  12.7 us
  transfers between devices with their start and end apart: 7, of which 6 were waited for; matrix products, arithmetic and copies ran while one was open for 5% of the time, Pallas kernels for 0%

commit v1 on v0

v1 whole, which is shorter than its diff:
```python
import jax
import jax.numpy as jnp
from jax import lax
from jax.experimental import pallas as pl
from jax.experimental.pallas import tpu as pltpu
from jax.sharding import PartitionSpec as P

DR = 12
SLOTS = 4
TAPS = 41
BLK = 256
NPATCH = 32
GROUP = 4


def toeplitz_store(taps_row, matrix):
    rows = jnp.broadcast_to(taps_row, (16, 128))
    skew = pltpu.roll(rows, 0, 1, stride=1, stride_axis=0)
    zeros = jnp.zeros((16, 256), jnp.float32)
    wide = jnp.concatenate([zeros, skew, zeros], axis=1)
    for step in range(-9, 3):
        d = 16 * step
        lo = 256 + d + 20
        tile = wide[:, lo : lo + 128].astype(jnp.bfloat16)
        rb = -step
        if rb >= 0:
            matrix[16 * rb : 16 * rb + 16, 0:128] = tile
        rb = 8 - step
        if rb < 16:
            matrix[16 * rb : 16 * rb + 16, 128:256] = tile


def match_kernel(tile_ref, weight_ref, taps_ref, blocks_hbm, out_ref, bbuf, mats, sems):
    count = bbuf.shape[0]

    def fetch(g):
        return pltpu.make_async_copy(
            blocks_hbm.at[pl.ds(g * GROUP, GROUP)], bbuf.at[pl.ds(g * GROUP, GROUP)], sems.at[g]
        )

    for g in range(count // GROUP):
        fetch(g).start()
    mats[...] = jnp.zeros_like(mats)

    @pl.loop(0, out_ref.shape[0])
    def _(t):
        out_ref[t] = jnp.zeros((BLK, BLK), jnp.bfloat16)

    @pl.loop(0, count // GROUP)
    def _(g):
        fetch(g).wait()
        for n in range(GROUP):
            i = g * GROUP + n
            toeplitz_store(taps_ref[i, 0:1, :], mats.at[n % 2, 0])
            toeplitz_store(taps_ref[i, 1:2, :], mats.at[n % 2, 1])
            half = jnp.dot(
                mats[n % 2, 0], bbuf[i], preferred_element_type=jnp.float32
            ).astype(jnp.bfloat16)
            full = lax.dot_general(
                half, mats[n % 2, 1], (((1,), (1,)), ((), ())), preferred_element_type=jnp.float32
            ).astype(jnp.bfloat16)
            t = tile_ref[i]
            out_ref[t] = (out_ref[t].astype(jnp.float32) + weight_ref[i] * full.astype(jnp.float32)).astype(jnp.bfloat16)


def match_partials(tile, weight, taps, blocks):
    count = blocks.shape[0]
    return pl.pallas_call(
        match_kernel,
        out_shape=jax.ShapeDtypeStruct((NPATCH * SLOTS, BLK, BLK), jnp.bfloat16),
        in_specs=[
            pl.BlockSpec(memory_space=pltpu.SMEM),
            pl.BlockSpec(memory_space=pltpu.SMEM),
            pl.BlockSpec(memory_space=pltpu.VMEM),
            pl.BlockSpec(memory_space=pl.ANY),
        ],
        out_specs=pl.BlockSpec(memory_space=pltpu.VMEM),
        scratch_shapes=[
            pltpu.VMEM((count, BLK, BLK), jnp.bfloat16),
            pltpu.VMEM((2, 2, BLK, BLK), jnp.bfloat16),
            pltpu.SemaphoreType.DMA((count // GROUP,)),
        ],
        compiler_params=pltpu.CompilerParams(vmem_limit_bytes=40 << 20),
        name="match_partials",
    )(tile, weight, taps, blocks)


def split_dot(a, b, dims):
    return lax.dot_general(a, b, dims, precision=lax.Precision.HIGH, preferred_element_type=jnp.float32)


def banded(taps, rows, cols, start):
    offsets = (
        lax.broadcasted_iota(jnp.int32, (rows, cols), 1)
        - lax.broadcasted_iota(jnp.int32, (rows, cols), 0)
        + start
    )
    table = jnp.zeros((rows, cols), jnp.float32)
    for t in range(taps.shape[0]):
        table = table + jnp.where(offsets == t, taps[t], jnp.zeros((), jnp.float32))
    return table


def local(blocks, dest_patch, dest_slot, weights, psf_taps, det_taps, noise_var):
    tile = dest_patch[0] * SLOTS + dest_slot[0]
    weight = weights[0].astype(jnp.float32)
    taps = jnp.pad(psf_taps[0].astype(jnp.float32), ((0, 0), (0, 0), (0, 128 - TAPS)))
    hits = jnp.where(tile[:, None] == jnp.arange(NPATCH * SLOTS, dtype=jnp.int32)[None, :], weight[:, None], 0.0)
    weight_part = jnp.sum(hits, axis=0).reshape(NPATCH, SLOTS)
    weight_sum = lax.psum_scatter(weight_part, "patch", scatter_dimension=0, tiled=True)[0]
    partial = match_partials(tile, weight, taps, blocks[0])
    total = lax.psum_scatter(partial, "patch", scatter_dimension=0, tiled=True)
    values = total.astype(jnp.float32) / jnp.maximum(weight_sum, 1.0)[:, None, None]
    image = values.reshape(2, 2, BLK, BLK).transpose(0, 2, 1, 3).reshape(2 * BLK, 2 * BLK)
    size = NPATCH
    up = [(i, (i + 1) % size) for i in range(size)]
    down = [(j, i) for i, j in up]
    before = lax.ppermute(image[:, -DR:], "patch", up)
    after = lax.ppermute(image[:, :DR], "patch", down)
    padded = jnp.concatenate([before, image, after], axis=1)
    kernel = det_taps[0]
    col_table = banded(kernel, 2 * BLK, 2 * BLK + 2 * DR, 0)
    row_table = banded(kernel, 2 * BLK, 2 * BLK, DR)
    col_pass = split_dot(padded, col_table, (((1,), (1,)), ((), ())))
    row_pass = split_dot(row_table, col_pass, (((1,), (0,)), ((), ())))
    term = row_pass * row_pass / noise_var[0]
    chi = lax.psum_scatter(term, "band", scatter_dimension=0, tiled=True)
    return image[None], chi


def solution(mesh):
    in_specs = (
        P("band", "patch", None, None),
        P("band", "patch"),
        P("band", "patch"),
        P("band", "patch"),
        P("band", "patch", None, None),
        P("band", None),
        P("band"),
    )
    out_specs = (P("band", None, "patch"), P("band", "patch"))
    return jax.shard_map(local, mesh=mesh, in_specs=in_specs, out_specs=out_specs, check_vma=False)
```

time: 497 us -> 238 us (0.48)
  waiting for transfers between devices: 300 us -> 25.4 us
  blocking collectives: 0 us -> 132 us
  matrix products: 109 us -> 38.1 us
  local copies, waits for them, and re-layouts: 39.1 us -> 7.44 us
  starting transfers between devices: 29.1 us -> 0.65 us
  Pallas kernels: 0 us -> 15.1 us
    all_to_all x4 -> x0, waiting for transfers between devices: 248 us -> none  [the longest x1 238 us: local(): lax.all_to_all(block_buffer, 'patch', split_axis=0, concat_axis=0, tiled=...]
    unnamed x0 -> x1, blocking collectives: none -> 132 us
    dot_general x19 -> x2, matrix products: 109 us -> 38.1 us  [split_dot(): lax.dot_general(a, b, dims, precision=lax.Precision.HIGH, preferred_eleme...]
    all_to_all x4 -> x0, starting transfers between devices: 23.9 us -> none  [the longest x1 8.42 us: local(): lax.all_to_all(weight_buffer, 'patch', split_axis=0, concat_axis=0, tiled...]
    ppermute x2, waiting for transfers between devices: 24.3 us -> 7.37 us  [the longest x1 5.3 us: local(): before = lax.ppermute(image[:, -DR:], 'patch', up)]
    scatter x4 -> x0, local copies, waits for them, and re-layouts: 15.8 us -> none  [the longest x1 11.3 us: local(): block_buffer = jnp.zeros((total_slots, block_edge, block_edge), jnp.bfloa...]
    pallas_call x0 -> x1, Pallas kernels: none -> 15.1 us  [match_partials(): pl.pallas_call(match_kernel, out_shape=jax.ShapeDtypeStruct((NPATCH * SLO...]
    squeeze x9 -> x0, local copies, waits for them, and re-layouts: 12.8 us -> none  [the longest x8 12.7 us: match_group(): matrices[:, 0]]
  transfers between devices with their start and end apart: 7 -> 4, of which waited for: 6 -> 3; matrix products, arithmetic and copies ran while one was open for 5% -> 2% of each run, Pallas kernels for 0% -> 0%
where the time goes in v1:
time: 238 us; the launch traced here: 237 us
  blocking collectives  132 us (55%)
  matrix products  38.1 us (16%)
  waiting for transfers between devices  25.4 us (11%)
  Pallas kernels  15.1 us (6%)
  between operations  14.8 us (6%)
  local copies, waits for them, and re-layouts  7.44 us (3%)
  other arithmetic  4.01 us (2%)
    unnamed x1, blocking collectives  132 us
    dot_general x2, matrix products, split_dot(): lax.dot_general(a, b, dims, precision=lax.Precision.HIGH, preferred_eleme...  38.1 us
    reduce_scatter x1, waiting for transfers between devices, local(): chi = lax.psum_scatter(term, 'band', scatter_dimension=0, tiled=True)  18 us
    pallas_call x1, Pallas kernels, match_partials(): pl.pallas_call(match_kernel, out_shape=jax.ShapeDtypeStruct((NPATCH * SLO...  15.1 us
    ppermute x1, waiting for transfers between devices, local(): before = lax.ppermute(image[:, -DR:], 'patch', up)  5.3 us
  transfers between devices with their start and end apart: 4, of which 3 were waited for; matrix products, arithmetic and copies ran while one was open for 2% of the time, Pallas kernels for 0%

profile of v1, /device:TPU:0, one launch (start us, length us, event | category | flops | bytes accessed | tf_op | source)
XLA Modules:
  0.0 237.1 jit_solution(14183605674082256242)
XLA Ops:
  7.2 0.0 reduce-scatter.3.cloned.1.call-start
  7.2 0.7 bitcast_convert_fusion.weight_ref
  7.9 0.7 pad_convert_fusion.taps_ref
  8.6 0.7 add_bitcast_fusion.tile_ref
  9.3 0.0 copy-start
  9.3 2.2 copy-done
  11.5 15.1 %match_partials.1 = bf16[128,256,256]{2,1,0:T(8,128)(2,1)} custom-call(s32[32]{0:T(128)S(1)} %add_bitcast_fusion.tile_ref, f32[32]{0:T(128)S(1)} %bitcast_convert_fusion.weight_ref, f32[32,2,128]{2,1,0:T(2,128)S(1)} %pad_convert_fusion.taps_ref, bf16[32,256,256]{2,1,0:T(8,128)(2,1)S(1)} %bitcast.44), custom_call_target="tpu_custom_call" | custom-call | tf_op jit(solution)/shard_map/match_partials/pallas_call | solution.py:68
  26.6 0.0 copy-start.2
  26.6 0.0 copy-start.1
  26.6 0.0 reduce-scatter.3.cloned.1.call-update
  26.6 0.0 reduce-scatter.5.cloned.1.call-start
  26.7 0.1 select_reduce_fusion
  26.8 0.1 reshape.92
  26.9 0.3 copy-done.2
  27.2 0.6 dynamic-slice
  27.8 131.6 %all-reduce.1 = f32[32,4]{1,0:T(8,128)S(1)} all-reduce(f32[32,4]{1,0:T(8,128)S(1)} %reshape.92), channel_id=3, replica_groups=mesh['patch'=32,'band'=4] {'patch'}, use_global_device_ids=true, to_apply=%region_2.3.clone | all-reduce | flops 128 | bytes 1024
  159.4 0.7 fusion.307
  160.1 0.0 copy-done.1
  160.1 0.7 fusion.363
  160.8 0.0 reduce-scatter.3.cloned.1.call-done
  160.8 1.2 convert_divide_fusion
  162.0 0.8 copy.16
  162.8 0.1 copy.13
  162.9 0.1 fusion.361
  163.1 0.1 collective-permute-start.1
  163.2 0.5 collective-permute-start
  163.7 0.7 fusion.364
  165.0 2.1 collective-permute-done.1
  167.0 5.3 %collective-permute-done = f32[512,12]{1,0:T(8,128)S(1)} collective-permute-done((f32[512,12]{1,0:T(8,128)S(1)}, f32[512,12]{1,0:T(8,128)S(1)}, u32[]{:S(2)}, u32[]{:S(2)}) %collective-permute-start) | collective-permute-done | bytes 24608 | tf_op jit(solution)/shard_map/ppermute | solution.py:118
  172.3 17.5 %fusion.1 = f32[512,512]{1,0:T(8,128)S(1)} fusion(f32[512,12]{1,0:T(8,128)S(1)} %collective-permute-done.1, f32[512,512]{1,0:T(8,128)S(1)} %bitcast.49, f32[512,12]{1,0:T(8,128)S(1)} %collective-permute-done, f32[]{:T(128)} %bitcast.32, f32[]{:T(128)} %bitcast.31, f32[]{:T(128)} %bitcast.30, f32[]{:T(128)} %bitcast.29, f32[]{:T(128)} %bitcast.28, ...), kind=kOutput, calls=%fused_computation.2 | convolution fusion | flops 864186368 | bytes 2146404 | tf_op jit(solution)/shard_map/dot_general | solution.py:89
  189.8 20.6 %fusion = f32[512,512]{1,0:T(8,128)} fusion(f32[512,512]{1,0:T(8,128)S(1)} %fusion.1, f32[]{:T(128)} %bitcast.43, f32[]{:T(128)} %bitcast.32, f32[]{:T(128)} %bitcast.31, f32[]{:T(128)} %bitcast.30, f32[]{:T(128)} %bitcast.29, f32[]{:T(128)} %bitcast.28, f32[]{:T(128)} %bitcast.27, f32[]{:T(128)} %bitcast.26, f32[]{:T(128)} %bitcast.25, f32[]{:T(128)} %bitcast.24, ...), kind=kOutput, calls=%fused_computation.1 | convolution fusion | flops 825753600 | bytes 2097256 | tf_op jit(solution)/shard_map/dot_general | solution.py:89
  210.4 0.0 reduce-scatter.5.cloned.1.call-update
  210.5 1.8 broadcast_in_dim_reshape.3
  212.3 18.0 %reduce-scatter.5.cloned.1.call-done = f32[128,512]{1,0:T(8,128)} async-done(((f32[512,512]{1,0:T(8,128)}), f32[128,512]{1,0:T(8,128)}) %reduce-scatter.5.cloned.1.call-update) | async-done | bytes 262160 | tf_op jit(solution)/shard_map/reduce_scatter | solution.py:127
Async XLA Ops:
  7.2 153.7 %reduce-scatter.3.cloned.1.call-start = ((), (), s32[]{:S(2)}) async-start(), calls=%async_computation.2 | async-start | bytes 17301504 | tf_op jit(solution)/shard_map/reduce_scatter | solution.py:112
  9.3 2.2 copy-start
  26.6 0.7 copy-start.2
  26.6 133.5 %copy-start.1 = (f32[1,25]{1,0:T(1,128)S(1)}, f32[1,25]{1,0:T(1,128)}, u32[]{:S(2)}) copy-start(f32[1,25]{1,0:T(1,128)} %param.12) | copy-start | bytes 304
  26.6 203.6 %reduce-scatter.5.cloned.1.call-start = ((), (), s32[]{:S(2)}) async-start(), calls=%async_computation.3 | async-start | bytes 1310720 | tf_op jit(solution)/shard_map/reduce_scatter | solution.py:127
  163.1 4.0 %collective-permute-start.1 = (f32[512,12]{1,0:T(8,128)S(1)}, f32[512,12]{1,0:T(8,128)S(1)}, u32[]{:S(2)}, u32[]{:S(2)}) collective-permute-start(f32[512,12]{1,0:T(8,128)S(1)} %get-tuple-element.3), channel_id=1, source_target_pairs={{4,0},{8,4},{12,8},{16,12},{20,16},{24,20},{28,24},{32,28},{36,32}... | collective-permute-start | bytes 73736 | tf_op jit(solution)/shard_map/ppermute | solution.py:119
  163.2 9.2 %collective-permute-start = (f32[512,12]{1,0:T(8,128)S(1)}, f32[512,12]{1,0:T(8,128)S(1)}, u32[]{:S(2)}, u32[]{:S(2)}) collective-permute-start(f32[512,12]{1,0:T(8,128)S(1)} %get-tuple-element.2), channel_id=1, source_target_pairs={{0,4},{4,8},{8,12},{12,16},{16,20},{20,24},{24,28},{28,32},{32,36}... | collective-permute-start | bytes 73736 | tf_op jit(solution)/shard_map/ppermute | solution.py:118
Sparse Core Ops, SparseCore 0:
  26.7 118.2 reduce-scatter.2
  210.6 19.5 reduce-scatter.4

commit v2 on v1

v2 whole, which is shorter than its diff:
```python
import jax
import jax.numpy as jnp
from jax import lax
from jax.experimental import pallas as pl
from jax.experimental.pallas import tpu as pltpu
from jax.sharding import PartitionSpec as P

DR = 12
DTAPS = 25
SLOTS = 4
TAPS = 41
BLK = 256
PH = 512
NPATCH = 32
NBAND = 4
SIDE = 4
GROUP = 4
STREAMS = ((1, 1), (1, -1), (0, 1), (0, -1))
BF16 = jnp.bfloat16
F32 = jnp.float32


def toeplitz_store(taps_row, matrix):
    rows = jnp.broadcast_to(taps_row, (16, 128))
    skew = pltpu.roll(rows, 0, 1, stride=1, stride_axis=0)
    zeros = jnp.zeros((16, 256), F32)
    wide = jnp.concatenate([zeros, skew, zeros], axis=1)
    for step in range(-9, 3):
        lo = 256 + 16 * step + 20
        tile = wide[:, lo : lo + 128].astype(BF16)
        rb = -step
        if rb >= 0:
            matrix[16 * rb : 16 * rb + 16, 0:128] = tile
        rb = 8 - step
        if rb < 16:
            matrix[16 * rb : 16 * rb + 16, 128:256] = tile


def match_kernel(tile_ref, weight_ref, taps_ref, blocks_ref, out_ref, mats):
    count = blocks_ref.shape[0]
    mats[...] = jnp.zeros_like(mats)

    @pl.loop(0, out_ref.shape[0])
    def _(t):
        out_ref[t] = jnp.zeros((BLK, BLK), BF16)

    @pl.loop(0, count // GROUP)
    def _(g):
        for n in range(GROUP):
            for axis in range(2):
                toeplitz_store(taps_ref[g * GROUP + n, axis : axis + 1, :], mats.at[n, axis])
        halves = []
        for n in range(GROUP):
            half = jnp.dot(mats[n, 0], blocks_ref[g * GROUP + n], preferred_element_type=F32)
            halves.append(half.astype(BF16))
        for n in range(GROUP):
            i = g * GROUP + n
            full = jnp.dot(halves[n], mats[n, 1], preferred_element_type=F32).astype(BF16)
            t = tile_ref[i]
            out_ref[t] = (out_ref[t].astype(F32) + weight_ref[i] * full.astype(F32)).astype(BF16)


def match_partials(tile, weight, taps, blocks):
    smem = pl.BlockSpec(memory_space=pltpu.SMEM)
    vmem = pl.BlockSpec(memory_space=pltpu.VMEM)
    return pl.pallas_call(
        match_kernel,
        out_shape=pltpu.VMEM((NPATCH * SLOTS, BLK, BLK), BF16),
        in_specs=[smem, smem, vmem, vmem],
        out_specs=vmem,
        scratch_shapes=[pltpu.VMEM((GROUP, 2, BLK, BLK), BF16)],
        compiler_params=pltpu.CompilerParams(vmem_limit_bytes=40 << 20),
        name="match_partials",
    )(tile, weight, taps, blocks)


def wrap(x):
    return lax.rem(x + 2 * SIDE, SIDE)


def patch_index(y, z, core):
    return (y * SIDE + z) * 2 + core


def split(x):
    high = x.astype(BF16)
    return high, (x - high.astype(F32)).astype(BF16)


def dot3(ah, al, bh, bl):
    dot = lambda a, b: jnp.dot(a, b, preferred_element_type=F32)
    return dot(ah, bh) + (dot(ah, bl) + dot(al, bh))


def tap_block(det_ref, shift, sign):
    offset = lax.broadcasted_iota(jnp.int32, (128, 128), 1) - lax.broadcasted_iota(jnp.int32, (128, 128), 0)
    offset = sign * offset + shift + DR
    block = jnp.zeros((128, 128), F32)
    for t in range(DTAPS):
        block = jnp.where(offset == t, det_ref[t], block)
    return block


def build_tables(det_ref, col_tab, row_tab):
    col_tab[...] = jnp.zeros_like(col_tab)
    row_tab[...] = jnp.zeros_like(row_tab)
    for table, sign in ((row_tab, 1), (col_tab, -1)):
        for diag in (-1, 0, 1):
            high, low = split(tap_block(det_ref, sign * 128 * diag, sign))
            for rb in range(PH // 128):
                cb = rb + diag
                if 0 <= cb < PH // 128:
                    table[0, 128 * rb : 128 * rb + 128, 128 * cb : 128 * cb + 128] = high
                    table[1, 128 * rb : 128 * rb + 128, 128 * cb : 128 * cb + 128] = low


def reduce_kernel(
    d_ref, w_ref, det_ref, noise_ref, img_ref, chi_ref,
    pair, hop1, hop2, w_in, halo_out, halo_in, col_tab, row_tab, high, low, term_own, term_out, term_in,
    pair_sem, hop1_sem, hop2_sem, send_sem, w_sem, halo_sem, term_sem,
):
    me = lax.axis_index("patch")
    band = lax.axis_index("band")
    core = lax.rem(me, 2)
    place = (lax.div(me, 2 * SIDE), lax.rem(lax.div(me, 2), SIDE))
    partner = me + 1 - 2 * core

    barrier = pltpu.get_barrier_semaphore()

    def greet(axis, device):
        pl.semaphore_signal(barrier, inc=1, device_id={axis: device})

    @pl.loop(1, NPATCH)
    def _(k):
        greet("patch", lax.rem(me + k, NPATCH))

    for k in range(1, NBAND):
        greet("band", lax.rem(band + k, NBAND))
    pl.semaphore_wait(barrier, NPATCH - 1 + NBAND - 1)

    def remote(src, dst, send, recv, device, axis="patch"):
        return pltpu.make_async_remote_copy(
            src_ref=src, dst_ref=dst, send_sem=send, recv_sem=recv, device_id={axis: device}
        )

    def dest(s, h, k, parity):
        axis, step = STREAMS[s]
        first = wrap(place[axis] - step * (1 + h))
        other = wrap(place[1 - axis] - step * (1 + k))
        y, z = (first, other) if axis == 0 else (other, first)
        return patch_index(y, z, parity) * SLOTS + s

    def neighbour(s, stage):
        axis, step = STREAMS[s]
        axis = axis if stage == 1 else 1 - axis
        moved = list(place)
        moved[axis] = wrap(place[axis] + step)
        return patch_index(moved[0], moved[1], core)

    next1 = [neighbour(s, 1) for s in range(SLOTS)]
    next2 = [neighbour(s, 2) for s in range(SLOTS)]

    def send_pair(s, h, k):
        remote(
            d_ref.at[dest(s, h, k, 1 - core)], pair.at[s, h, k], send_sem.at[0], pair_sem.at[s, h, k], partner
        ).start()

    def wait_pair(s, h, k):
        remote(pair.at[s, h, k], pair.at[s, h, k], send_sem.at[0], pair_sem.at[s, h, k], partner).wait_recv()

    def hop1_copy(s, h, k):
        return remote(pair.at[s, h, k], hop1.at[s, h, k], send_sem.at[1], hop1_sem.at[s, h, k], next1[s])

    def hop2_copy(s, k):
        return remote(pair.at[s, 3, k], hop2.at[s, k], send_sem.at[2], hop2_sem.at[s, k], next2[s])

    @pl.loop(0, SIDE)
    def _(k):
        for s in range(SLOTS):
            send_pair(s, 0, k)

    @pl.loop(1, NPATCH)
    def _(k):
        device = lax.rem(me + k, NPATCH)
        remote(w_ref.at[device], w_in.at[k - 1], send_sem.at[3], w_sem.at[0], device).start()

    def here(s, h, k):
        return d_ref[dest(s, h, k, core)].astype(F32) + pair[s, h, k].astype(F32)

    @pl.loop(0, SIDE)
    def _(k):
        for s in range(SLOTS):
            wait_pair(s, 0, k)
            pair[s, 0, k] = here(s, 0, k).astype(BF16)
            hop1_copy(s, 0, k).start()
            send_pair(s, 1, k)

    build_tables(det_ref, col_tab, row_tab)

    @pl.loop(1, SIDE - 1)
    def _(h):
        @pl.loop(0, SIDE)
        def _(k):
            for s in range(SLOTS):
                send_pair(s, h + 1, k)
            for s in range(SLOTS):
                wait_pair(s, h, k)
                hop1_copy(s, h - 1, k).wait_recv()
                pair[s, h, k] = (here(s, h, k) + hop1[s, h - 1, k].astype(F32)).astype(BF16)
                hop1_copy(s, h, k).start()

    def gathered(s, k):
        wait_pair(s, 3, k)
        hop1_copy(s, 2, k).wait_recv()
        return here(s, 3, k) + hop1[s, 2, k].astype(F32)

    for s in range(SLOTS):
        pair[s, 3, 0] = gathered(s, 0).astype(BF16)
        hop2_copy(s, 0).start()

    @pl.loop(1, SIDE - 1)
    def _(k):
        for s in range(SLOTS):
            total = gathered(s, k)
            hop2_copy(s, k - 1).wait_recv()
            pair[s, 3, k] = (total + hop2[s, k - 1].astype(F32)).astype(BF16)
            hop2_copy(s, k).start()

    all_w = remote(w_in, w_in, send_sem.at[3], w_sem.at[0], partner)
    all_w.wait_recv()
    weight_sum = w_ref[me]
    for k in range(NPATCH - 1):
        weight_sum = weight_sum + w_in[k]
    scale = jnp.maximum(weight_sum, 1.0)

    for s in range(SLOTS):
        total = gathered(s, 3)
        hop2_copy(s, 2).wait_recv()
        total = total + hop2[s, 2].astype(F32)
        divisor = jnp.broadcast_to(scale[s : s + 1, 0:1], (BLK, BLK))
        value = total / divisor
        rows = slice((s // 2) * BLK, (s // 2 + 1) * BLK)
        cols = slice((s % 2) * BLK, (s % 2 + 1) * BLK)
        img_ref[rows, cols] = value
        high[rows, cols], low[rows, cols] = split(value)

    halo_out[0] = high[:, 0:128]
    halo_out[1] = high[:, PH - 128 : PH]
    before = lax.rem(me + NPATCH - 1, NPATCH)
    after = lax.rem(me + 1, NPATCH)
    to_before = remote(halo_out.at[0], halo_in.at[1], send_sem.at[4], halo_sem.at[1], before)
    to_after = remote(halo_out.at[1], halo_in.at[0], send_sem.at[5], halo_sem.at[0], after)
    to_before.start()
    to_after.start()
    col = dot3(high[...], low[...], col_tab[0], col_tab[1])
    to_before.wait_recv()
    to_after.wait_recv()
    dot = lambda a, b: jnp.dot(a, b, preferred_element_type=F32)
    left = halo_in[0]
    right = halo_in[1]
    from_left = dot(left, col_tab[0, 0:128, 128:256]) + dot(left, col_tab[1, 0:128, 128:256])
    from_right = dot(right, col_tab[0, 128:256, 0:128]) + dot(right, col_tab[1, 128:256, 0:128])
    col = jnp.concatenate(
        [col[:, 0:128] + from_left, col[:, 128 : PH - 128], col[:, PH - 128 : PH] + from_right], axis=1
    )
    high[...], low[...] = split(col)
    row = dot3(row_tab[0], row_tab[1], high[...], low[...])
    term = row * row / noise_ref[0]
    height = PH // NBAND
    for g in range(NBAND):
        part = term[g * height : (g + 1) * height]
        term_own[g] = part
        term_out[g] = part.astype(BF16)

    def term_copy(k):
        target = lax.rem(band + k, NBAND)
        return remote(
            term_out.at[target], term_in.at[k - 1], send_sem.at[5 + k], term_sem.at[k - 1], target, "band"
        )

    for k in range(1, NBAND):
        term_copy(k).start()
    chi = term_own[band]
    for k in range(1, NBAND):
        term_copy(k).wait_recv()
        chi = chi + term_in[k - 1].astype(F32)
    chi_ref[...] = chi

    for index, ref in enumerate((pair, hop1, hop2, w_in)):
        remote(ref, ref, send_sem.at[index], w_sem.at[0], partner).wait_send()
    to_before.wait_send()
    to_after.wait_send()
    for k in range(1, NBAND):
        term_copy(k).wait_send()


def reduce_partials(partial, weight_table, det_taps, noise_var):
    smem = pl.BlockSpec(memory_space=pltpu.SMEM)
    vmem = pl.BlockSpec(memory_space=pltpu.VMEM)
    dma = pltpu.SemaphoreType.DMA
    height = PH // NBAND
    return pl.pallas_call(
        reduce_kernel,
        out_shape=(
            jax.ShapeDtypeStruct((PH, PH), F32),
            jax.ShapeDtypeStruct((height, PH), F32),
        ),
        in_specs=[vmem, vmem, smem, smem],
        out_specs=(vmem, vmem),
        scratch_shapes=[
            pltpu.VMEM((SLOTS, SIDE, SIDE, BLK, BLK), BF16),
            pltpu.VMEM((SLOTS, SIDE - 1, SIDE, BLK, BLK), BF16),
            pltpu.VMEM((SLOTS, SIDE - 1, BLK, BLK), BF16),
            pltpu.VMEM((NPATCH - 1, 8, 128), F32),
            pltpu.VMEM((2, PH, 128), BF16),
            pltpu.VMEM((2, PH, 128), BF16),
            pltpu.VMEM((2, PH, PH), BF16),
            pltpu.VMEM((2, PH, PH), BF16),
            pltpu.VMEM((PH, PH), BF16),
            pltpu.VMEM((PH, PH), BF16),
            pltpu.VMEM((NBAND, height, PH), F32),
            pltpu.VMEM((NBAND, height, PH), BF16),
            pltpu.VMEM((NBAND - 1, height, PH), BF16),
            dma((SLOTS, SIDE, SIDE)),
            dma((SLOTS, SIDE - 1, SIDE)),
            dma((SLOTS, SIDE - 1)),
            dma((9,)),
            dma((1,)),
            dma((2,)),
            dma((NBAND - 1,)),
        ],
        compiler_params=pltpu.CompilerParams(
            vmem_limit_bytes=48 << 20, collective_id=0, has_side_effects=True
        ),
        name="reduce_partials",
    )(partial, weight_table, det_taps, noise_var)


def local(blocks, dest_patch, dest_slot, weights, psf_taps, det_taps, noise_var):
    tile = dest_patch[0] * SLOTS + dest_slot[0]
    weight = weights[0].astype(F32)
    taps = psf_taps[0].astype(F32)
    taps = jnp.stack([taps[:, 0], taps[:, 1, ::-1]], axis=1)
    taps = jnp.pad(taps, ((0, 0), (0, 0), (0, 128 - TAPS)))
    slots = jnp.arange(NPATCH * 8, dtype=jnp.int32)
    slots = jnp.where(slots % 8 < SLOTS, slots // 8 * SLOTS + slots % 8, -1)
    hits = jnp.where(tile[:, None] == slots[None, :], weight[:, None], 0.0)
    weight_table = jnp.broadcast_to(jnp.sum(hits, axis=0).reshape(NPATCH, 8, 1), (NPATCH, 8, 128))
    partial = match_partials(tile, weight, taps, blocks[0])
    image, chi = reduce_partials(partial, weight_table, det_taps[0], noise_var)
    return image[None], chi


def solution(mesh):
    in_specs = (
        P("band", "patch", None, None),
        P("band", "patch"),
        P("band", "patch"),
        P("band", "patch"),
        P("band", "patch", None, None),
        P("band", None),
        P("band"),
    )
    out_specs = (P("band", None, "patch"), P("band", "patch"))
    return jax.shard_map(local, mesh=mesh, in_specs=in_specs, out_specs=out_specs, check_vma=False)
```

time: 238 us -> 101 us (0.42)
  blocking collectives: 132 us -> 0 us
  Pallas kernels: 15.1 us -> 88.4 us
  matrix products: 38.1 us -> 0 us
  waiting for transfers between devices: 25.4 us -> 0 us
  between operations: 14.8 us -> 1.36 us
    unnamed x1 -> x0, blocking collectives: 132 us -> none
    pallas_call x1 -> x2, Pallas kernels: 15.1 us -> 88.4 us  [the longest x1 78.8 us: reduce_partials(): pl.pallas_call(reduce_kernel, out_shape=(jax.ShapeDtypeStruct((PH, PH), F...]
    dot_general x2 -> x0, matrix products: 38.1 us -> none  [split_dot(): lax.dot_general(a, b, dims, precision=lax.Precision.HIGH, preferred_eleme...]
    reduce_scatter x2 -> x0, waiting for transfers between devices: 18 us -> none  [the longest x1 18 us: local(): chi = lax.psum_scatter(term, 'band', scatter_dimension=0, tiled=True)]
    ppermute x2 -> x0, waiting for transfers between devices: 7.37 us -> none  [the longest x1 5.3 us: local(): before = lax.ppermute(image[:, -DR:], 'patch', up)]
    unnamed x8 -> x10, local copies, waits for them, and re-layouts: 3.2 us -> 7.41 us
  transfers between devices with their start and end apart: 4 -> 0, of which waited for: 3 -> 0; matrix products, arithmetic and copies ran while one was open for 2% -> 0% of each run, Pallas kernels for 0% -> 0%
where the time goes in v2:
time: 101 us; the launch traced here: 100 us
  Pallas kernels  88.4 us (88%)
  local copies, waits for them, and re-layouts  7.73 us (8%)
  other arithmetic  2.84 us (3%)
  between operations  1.36 us (1%)
    pallas_call x1, Pallas kernels, reduce_partials(): pl.pallas_call(reduce_kernel, out_shape=(jax.ShapeDtypeStruct((PH, PH), F...  78.8 us
    pallas_call x1, Pallas kernels, match_partials(): pl.pallas_call(match_kernel, out_shape=pltpu.VMEM((NPATCH * SLOTS, BLK, B...  9.63 us
    unnamed x10, local copies, waits for them, and re-layouts  7.41 us

profile of v2, /device:TPU:0, one launch (start us, length us, event | category | flops | bytes accessed | tf_op | source)
XLA Modules:
  0.0 100.4 jit_solution(2244314995066060951)
XLA Ops:
  0.6 0.0 copy-start.1
  1.3 0.7 add_bitcast_fusion.tile_ref
  2.0 0.0 copy-start.2
  2.0 0.7 bitcast_convert_fusion.1.weight_ref
  2.6 0.0 copy-start.3
  2.6 0.1 select_reduce_fusion
  2.7 0.1 broadcast_in_dim.29
  2.8 0.7 bitcast_convert_fusion
  3.6 0.1 rev.3
  3.7 0.7 select_maximum_fusion.taps_ref
  4.4 0.1 broadcast_in_dim.30.w_ref
  4.5 0.0 copy-done.2
  4.5 0.0 copy-done.3
  4.5 9.6 %match_partials.1.d_ref = bf16[128,256,256]{2,1,0:T(8,128)(2,1)S(1)} custom-call(s32[32]{0:T(128)} %copy-done.2, f32[32]{0:T(128)} %copy-done.3, f32[32,2,128]{2,1,0:T(2,128)} %select_maximum_fusion.taps_ref, bf16[32,256,256]{2,1,0:T(8,128)(2,1)} %bitcast.13), custom_call_target="tpu_custom_call" | custom-call | tf_op jit(solution)/shard_map/match_partials/pallas_call | solution.py:66
  14.2 0.0 copy-start
  14.2 5.7 %copy-done = bf16[128,256,256]{2,1,0:T(8,128)(2,1)} copy-done((bf16[128,256,256]{2,1,0:T(8,128)(2,1)}, bf16[128,256,256]{2,1,0:T(8,128)(2,1)S(1)}, u32[]{:S(2)}) %copy-start) | copy-done | bytes 16777240
  19.9 0.0 copy-done.1
  19.9 78.8 %reduce_partials.1 = (f32[512,512]{1,0:T(8,128)S(1)}, f32[128,512]{1,0:T(8,128)S(1)}) custom-call(bf16[128,256,256]{2,1,0:T(8,128)(2,1)} %copy-done, f32[32,8,128]{2,1,0:T(8,128)S(1)} %broadcast_in_dim.30.w_ref, f32[25]{0:T(128)S(1)} %bitcast.12, f32[1]{0:T(128)S(6)} %copy.11.noise_ref), custom_call_target="tpu_custom_call" | custom-call | tf_op jit(solution)/shard_map/reduce_partials/pallas_call | solution.py:302
  98.7 1.0 copy.12
  99.7 0.7 copy.13
  (2 shorter events, 0.0 us)
Async XLA Ops:
  0.6 19.3 %copy-start.1 = (f32[1,25]{1,0:T(1,128)S(1)}, f32[1,25]{1,0:T(1,128)}, u32[]{:S(2)}) copy-start(f32[1,25]{1,0:T(1,128)} %param.12) | copy-start | bytes 304
  2.0 2.5 %copy-start.2 = (s32[32]{0:T(128)}, s32[32]{0:T(128)S(1)}, u32[]{:S(2)}) copy-start(s32[32]{0:T(128)S(1)} %add_bitcast_fusion.tile_ref) | copy-start | bytes 388
  2.6 1.9 %copy-start.3 = (f32[32]{0:T(128)}, f32[32]{0:T(128)S(1)}, u32[]{:S(2)}) copy-start(f32[32]{0:T(128)S(1)} %bitcast_convert_fusion.1.weight_ref) | copy-start | bytes 388
  14.2 5.7 %copy-start = (bf16[128,256,256]{2,1,0:T(8,128)(2,1)}, bf16[128,256,256]{2,1,0:T(8,128)(2,1)S(1)}, u32[]{:S(2)}) copy-start(bf16[128,256,256]{2,1,0:T(8,128)(2,1)S(1)} %match_partials.1.d_ref) | copy-start | bytes 50331652

commit v3 on v2

v3 whole, which is shorter than its diff:
```python
import jax
import jax.numpy as jnp
from jax import lax
from jax.experimental import pallas as pl
from jax.experimental.pallas import tpu as pltpu
from jax.sharding import PartitionSpec as P

DR = 12
DTAPS = 25
SLOTS = 4
TAPS = 41
BLK = 256
PH = 512
NPATCH = 32
NBAND = 4
SIDE = 4
GROUP = 4
STREAMS = ((1, 1), (1, -1), (0, 1), (0, -1))
BF16 = jnp.bfloat16
F32 = jnp.float32


def toeplitz_store(taps_row, matrix):
    rows = jnp.broadcast_to(taps_row, (16, 128))
    skew = pltpu.roll(rows, 0, 1, stride=1, stride_axis=0)
    zeros = jnp.zeros((16, 256), F32)
    wide = jnp.concatenate([zeros, skew, zeros], axis=1)
    for step in range(-9, 3):
        lo = 256 + 16 * step + 20
        tile = wide[:, lo : lo + 128].astype(BF16)
        rb = -step
        if rb >= 0:
            matrix[16 * rb : 16 * rb + 16, 0:128] = tile
        rb = 8 - step
        if rb < 16:
            matrix[16 * rb : 16 * rb + 16, 128:256] = tile


def match_kernel(
    patch_hbm, slot_hbm, weight_hbm, taps_ref, blocks_hbm, out_ref,
    patch_ref, slot_ref, weight_ref, blocks, table_ref, tap_rows, weight_rows, mats, sems, small_sems,
):
    count = blocks.shape[0]

    def fetch(g):
        part = pl.ds(g * GROUP, GROUP)
        return pltpu.make_async_copy(blocks_hbm.at[0, part], blocks.at[part], sems.at[g])

    small = [
        pltpu.make_async_copy(src, dst, small_sems.at[n])
        for n, (src, dst) in enumerate(((weight_hbm, weight_ref), (patch_hbm, patch_ref), (slot_hbm, slot_ref)))
    ]
    for copy in small:
        copy.start()
    for g in range(count // GROUP):
        fetch(g).start()
    mats[...] = jnp.zeros_like(mats)
    table_ref[...] = jnp.zeros_like(table_ref)
    tap_rows[0] = taps_ref[0].astype(F32)
    ends = lax.broadcasted_iota(jnp.int32, (128, 128), 0) + lax.broadcasted_iota(jnp.int32, (128, 128), 1)
    reverse = jnp.where(ends == TAPS - 1, 1.0, 0.0).astype(BF16)
    tap_rows[1] = jnp.dot(taps_ref[1], reverse, preferred_element_type=F32)
    for copy in small:
        copy.wait()
    diagonal = lax.broadcasted_iota(jnp.int32, (count, count), 0) == lax.broadcasted_iota(jnp.int32, (count, count), 1)
    spread = jnp.where(diagonal, jnp.broadcast_to(weight_ref[...].astype(F32), (count, count)), 0.0)
    weight_rows[...] = jnp.broadcast_to(jnp.sum(spread, axis=1, keepdims=True), (count, 128))

    @pl.loop(0, count // GROUP)
    def _(g):
        fetch(g).wait()
        for n in range(GROUP):
            for axis in range(2):
                toeplitz_store(tap_rows[axis, pl.ds(g * GROUP + n, 1), :], mats.at[n, axis])
        halves = []
        for n in range(GROUP):
            half = jnp.dot(mats[n, 0], blocks[g * GROUP + n], preferred_element_type=F32)
            halves.append(half.astype(BF16))
        for n in range(GROUP):
            i = g * GROUP + n
            full = jnp.dot(halves[n], mats[n, 1], preferred_element_type=F32).astype(BF16)
            weight = weight_rows[pl.ds(i, 1), :]
            patch = patch_ref[0, i]
            slot = slot_ref[0, i]
            place = (patch & 1) * (SIDE * SIDE) + ((patch >> 1) & (SIDE - 1)) * SIDE + (patch >> 3)
            before = table_ref[place, pl.ds(slot, 1), :]
            table_ref[place, pl.ds(slot, 1), :] = before + weight
            wide = lambda row: jnp.broadcast_to(jnp.concatenate([row, row], axis=1), (BLK, BLK))
            tile = patch * SLOTS + slot
            old = jnp.where(wide(before) > 0.0, out_ref[tile].astype(F32), 0.0)
            out_ref[tile] = (old + wide(weight) * full.astype(F32)).astype(BF16)

    high, low = split(table_ref[...].reshape(NPATCH * 8, 128))
    out_ref[NPATCH * SLOTS, :, 0:128] = high
    out_ref[NPATCH * SLOTS, :, 128:256] = low


def match_partials(blocks, dest_patch, dest_slot, weights, taps):
    count = blocks.shape[1]
    hbm = pl.BlockSpec(memory_space=pltpu.HBM)
    vmem = pl.BlockSpec(memory_space=pltpu.VMEM)
    keep = lambda x: pltpu.with_memory_space_constraint(x, pltpu.HBM)
    return pl.pallas_call(
        match_kernel,
        out_shape=pltpu.VMEM((NPATCH * SLOTS + 1, BLK, BLK), BF16),
        in_specs=[hbm, hbm, hbm, vmem, hbm],
        out_specs=vmem,
        scratch_shapes=[
            pltpu.SMEM((1, count), jnp.int32),
            pltpu.SMEM((1, count), jnp.int32),
            pltpu.VMEM((1, count), BF16),
            pltpu.VMEM((count, BLK, BLK), BF16),
            pltpu.VMEM((NPATCH, 8, 128), F32),
            pltpu.VMEM((2, count, 128), F32),
            pltpu.VMEM((count, 128), F32),
            pltpu.VMEM((GROUP, 2, BLK, BLK), BF16),
            pltpu.SemaphoreType.DMA((count // GROUP,)),
            pltpu.SemaphoreType.DMA((3,)),
        ],
        compiler_params=pltpu.CompilerParams(vmem_limit_bytes=28 << 20),
        name="match_partials",
    )(keep(dest_patch), keep(dest_slot), keep(weights), taps, keep(blocks))


def wrap(x):
    return lax.rem(x + 2 * SIDE, SIDE)


def patch_index(y, z, core):
    return (y * SIDE + z) * 2 + core


def split(x):
    high = x.astype(BF16)
    return high, (x - high.astype(F32)).astype(BF16)


def dot3(ah, al, bh, bl):
    dot = lambda a, b: jnp.dot(a, b, preferred_element_type=F32)
    return dot(ah, bh) + (dot(ah, bl) + dot(al, bh))


def tap_block(det_ref, shift, sign):
    offset = lax.broadcasted_iota(jnp.int32, (128, 128), 1) - lax.broadcasted_iota(jnp.int32, (128, 128), 0)
    offset = sign * offset + shift + DR
    block = jnp.zeros((128, 128), F32)
    for t in range(DTAPS):
        block = jnp.where(offset == t, det_ref[t], block)
    return block


def build_tables(det_ref, col_tab, row_tab):
    col_tab[...] = jnp.zeros_like(col_tab)
    row_tab[...] = jnp.zeros_like(row_tab)
    for table, sign in ((row_tab, 1), (col_tab, -1)):
        for diag in (-1, 0, 1):
            high, low = split(tap_block(det_ref, sign * 128 * diag, sign))
            for rb in range(PH // 128):
                cb = rb + diag
                if 0 <= cb < PH // 128:
                    table[0, 128 * rb : 128 * rb + 128, 128 * cb : 128 * cb + 128] = high
                    table[1, 128 * rb : 128 * rb + 128, 128 * cb : 128 * cb + 128] = low


def reduce_kernel(
    d_ref, det_ref, noise_ref, img_ref, chi_ref,
    pair, hop1, hop2, w_ref, w_pair, w_acc, w_hop1, w_hop2, halo_out, halo_in, col_tab, row_tab, high, low,
    term, far_out, far_in, near_out, near_in,
    pair_sem, hop1_sem, hop2_sem, send_sem, w_sem, halo_sem, far_sem, near_sem, end_sem,
):
    me = lax.axis_index("patch")
    band = lax.axis_index("band")
    core = lax.rem(me, 2)
    place = (lax.div(me, 2 * SIDE), lax.rem(lax.div(me, 2), SIDE))
    partner = me + 1 - 2 * core
    before = lax.rem(me + NPATCH - 1, NPATCH)
    after = lax.rem(me + 1, NPATCH)
    beside = lax.rem(me + NPATCH - 1 + 2 * core, NPATCH)

    def moved(axis, step):
        there = list(place)
        there[axis] = wrap(place[axis] + step)
        return patch_index(there[0], there[1], core)

    barrier = pltpu.get_barrier_semaphore()
    for device in (partner, beside, moved(0, 1), moved(0, -1), moved(1, 1), moved(1, -1)):
        pl.semaphore_signal(barrier, inc=1, device_id={"patch": device})
    above = lax.rem(band + 1, NBAND)
    below = lax.rem(band + NBAND - 1, NBAND)
    for device in (above, below):
        pl.semaphore_signal(barrier, inc=1, device_id={"band": device})
    pl.semaphore_wait(barrier, 8)

    def remote(src, dst, send, recv, device, axis="patch"):
        return pltpu.make_async_remote_copy(
            src_ref=src, dst_ref=dst, send_sem=send, recv_sem=recv, device_id={axis: device}
        )

    def dest(s, h, k):
        axis, step = STREAMS[s]
        first = wrap(place[axis] - step * (1 + h))
        other = wrap(place[1 - axis] - step * (1 + k))
        return (first, other) if axis == 0 else (other, first)

    def tile(s, h, k, parity):
        y, z = dest(s, h, k)
        return patch_index(y, z, parity) * SLOTS + s

    next1 = [moved(axis, step) for axis, step in STREAMS]
    next2 = [moved(1 - axis, step) for axis, step in STREAMS]

    def send_pair(s, h, k):
        remote(
            d_ref.at[tile(s, h, k, 1 - core)], pair.at[s, h, k], send_sem.at[0], pair_sem.at[s, h, k], partner
        ).start()

    def wait_pair(s, h, k):
        remote(pair.at[s, h, k], pair.at[s, h, k], send_sem.at[0], pair_sem.at[s, h, k], partner).wait_recv()

    def hop1_copy(s, h, k):
        return remote(pair.at[s, h, k], hop1.at[s, h, k], send_sem.at[1], hop1_sem.at[s, h, k], next1[s])

    def hop2_copy(s, k):
        return remote(pair.at[s, 3, k], hop2.at[s, k], send_sem.at[2], hop2_sem.at[s, k], next2[s])

    table = d_ref[NPATCH * SLOTS]
    table = table[:, 0:128].astype(F32) + table[:, 128:256].astype(F32)
    w_ref[...] = table.reshape(2, SIDE, SIDE, 8, 128)
    w_exchange = remote(w_ref.at[1 - core], w_pair, send_sem.at[3], w_sem.at[0], partner)
    w_exchange.start()

    @pl.loop(0, SIDE)
    def _(k):
        for s in range(SLOTS):
            send_pair(s, 0, k)

    w_exchange.wait_recv()

    def w_here(h):
        z = wrap(place[1] - 1 - h)
        return w_ref[core, z] + w_pair[z]

    def w_copy1(h):
        return remote(w_acc.at[h], w_hop1.at[h], send_sem.at[4 + h], w_sem.at[1 + h], moved(1, 1))

    def w_copy2(k):
        return remote(w_acc.at[3 + k], w_hop2.at[k], send_sem.at[7 + k], w_sem.at[4 + k], moved(0, 1))

    def here(s, h, k):
        y, z = dest(s, h, k)
        wide = lambda row: jnp.broadcast_to(jnp.concatenate([row, row], axis=1), (BLK, BLK))
        mine = jnp.where(
            wide(w_ref[core, z, y, s : s + 1]) > 0.0, d_ref[tile(s, h, k, core)].astype(F32), 0.0
        )
        other = jnp.where(wide(w_pair[z, y, s : s + 1]) > 0.0, pair[s, h, k].astype(F32), 0.0)
        return mine + other

    w_acc[0] = w_here(0)
    w_copy1(0).start()

    @pl.loop(0, SIDE)
    def _(k):
        for s in range(SLOTS):
            wait_pair(s, 0, k)
            pair[s, 0, k] = here(s, 0, k).astype(BF16)
            hop1_copy(s, 0, k).start()
            send_pair(s, 1, k)

    build_tables(det_ref, col_tab, row_tab)

    @pl.loop(1, SIDE - 1)
    def _(h):
        @pl.loop(0, SIDE)
        def _(k):
            for s in range(SLOTS):
                send_pair(s, h + 1, k)
            for s in range(SLOTS):
                wait_pair(s, h, k)
                total = here(s, h, k)
                hop1_copy(s, h - 1, k).wait_recv()
                pair[s, h, k] = (total + hop1[s, h - 1, k].astype(F32)).astype(BF16)
                hop1_copy(s, h, k).start()

        w_copy1(h - 1).wait_recv()
        w_acc[h] = w_here(h) + w_hop1[h - 1]
        w_copy1(h).start()

    def gathered(s, k):
        wait_pair(s, 3, k)
        hop1_copy(s, 2, k).wait_recv()
        return here(s, 3, k) + hop1[s, 2, k].astype(F32)

    for s in range(SLOTS):
        pair[s, 3, 0] = gathered(s, 0).astype(BF16)
        hop2_copy(s, 0).start()

    w_copy1(2).wait_recv()
    w_acc[3] = w_here(3) + w_hop1[2]
    w_copy2(0).start()

    @pl.loop(1, SIDE - 1)
    def _(k):
        for s in range(SLOTS):
            total = gathered(s, k)
            hop2_copy(s, k - 1).wait_recv()
            pair[s, 3, k] = (total + hop2[s, k - 1].astype(F32)).astype(BF16)
            hop2_copy(s, k).start()
        w_copy2(k - 1).wait_recv()
        w_acc[3 + k] = w_acc[3] + w_hop2[k - 1]
        w_copy2(k).start()

    w_copy2(2).wait_recv()
    weight_sum = w_acc[3, place[0]] + w_hop2[2, place[0]]
    scale = jnp.maximum(weight_sum, 1.0)

    for s in range(SLOTS):
        total = gathered(s, 3)
        hop2_copy(s, 2).wait_recv()
        total = total + hop2[s, 2].astype(F32)
        divisor = jnp.broadcast_to(scale[s : s + 1, 0:1], (BLK, BLK))
        value = total / divisor
        rows = slice((s // 2) * BLK, (s // 2 + 1) * BLK)
        cols = slice((s % 2) * BLK, (s % 2 + 1) * BLK)
        img_ref[rows, cols] = value
        high[rows, cols], low[rows, cols] = split(value)

    halo_out[0] = high[:, 0:128]
    halo_out[1] = high[:, PH - 128 : PH]
    to_before = remote(halo_out.at[0], halo_in.at[1], end_sem.at[0], halo_sem.at[1], before)
    to_after = remote(halo_out.at[1], halo_in.at[0], end_sem.at[1], halo_sem.at[0], after)
    to_before.start()
    to_after.start()
    high[...], low[...] = split(dot3(high[...], low[...], col_tab[0], col_tab[1]))
    row = dot3(row_tab[0], row_tab[1], high[...], low[...])
    to_before.wait_recv()
    to_after.wait_recv()
    dot = lambda a, b: jnp.dot(a, b, preferred_element_type=F32)
    left = halo_in[0]
    right = halo_in[1]
    from_left = dot(left, col_tab[0, 0:128, 128:256]) + dot(left, col_tab[1, 0:128, 128:256])
    from_right = dot(right, col_tab[0, 128:256, 0:128]) + dot(right, col_tab[1, 128:256, 0:128])
    edge_high, edge_low = split(jnp.concatenate([from_left, from_right], axis=1))
    edge = dot3(row_tab[0], row_tab[1], edge_high, edge_low)
    row = jnp.concatenate(
        [row[:, 0:128] + edge[:, 0:128], row[:, 128 : PH - 128], row[:, PH - 128 : PH] + edge[:, 128:256]],
        axis=1,
    )
    squares = row * row / noise_ref[0]
    height = PH // NBAND
    part = height // 2
    for g in range(NBAND):
        term[g] = squares[g * height : (g + 1) * height]
    opposite = lax.rem(band + 2, NBAND)
    near = (above, below)
    far_copy = lambda d: remote(far_out.at[d], far_in.at[d], end_sem.at[2 + d], far_sem.at[d], near[d], "band")
    near_copy = lambda d, n: remote(
        near_out.at[d, n], near_in.at[d, n], end_sem.at[4 + 2 * d + n], near_sem.at[2 * d + n], near[d], "band"
    )
    for d in range(2):
        far_out[d] = term[opposite, d * part : (d + 1) * part].astype(BF16)
        far_copy(d).start()
    for d in range(2):
        near_out[d, 1 - d] = term[near[d], (1 - d) * part : (2 - d) * part].astype(BF16)
        near_copy(d, 1 - d).start()
    for d in range(2):
        far_copy(d).wait_recv()
        near_out[d, d] = (term[near[d], d * part : (d + 1) * part] + far_in[d].astype(F32)).astype(BF16)
        near_copy(d, d).start()
    for n in range(2):
        near_copy(0, n).wait_recv()
        near_copy(1, n).wait_recv()
        own = term[band, n * part : (n + 1) * part]
        chi_ref[n * part : (n + 1) * part] = own + (near_in[0, n].astype(F32) + near_in[1, n].astype(F32))

    for index, ref in enumerate((pair, hop1, hop2)):
        remote(ref, ref, send_sem.at[index], w_sem.at[0], partner).wait_send()
    w_exchange.wait_send()
    for h in range(SIDE - 1):
        w_copy1(h).wait_send()
        w_copy2(h).wait_send()
    to_before.wait_send()
    to_after.wait_send()
    for d in range(2):
        far_copy(d).wait_send()
        for n in range(2):
            near_copy(d, n).wait_send()


def reduce_partials(partial, det_taps, noise_var):
    smem = pl.BlockSpec(memory_space=pltpu.SMEM)
    vmem = pl.BlockSpec(memory_space=pltpu.VMEM)
    dma = pltpu.SemaphoreType.DMA
    height = PH // NBAND
    return pl.pallas_call(
        reduce_kernel,
        out_shape=(
            jax.ShapeDtypeStruct((PH, PH), F32),
            jax.ShapeDtypeStruct((height, PH), F32),
        ),
        in_specs=[vmem, smem, smem],
        out_specs=(vmem, vmem),
        scratch_shapes=[
            pltpu.VMEM((SLOTS, SIDE, SIDE, BLK, BLK), BF16),
            pltpu.VMEM((SLOTS, SIDE - 1, SIDE, BLK, BLK), BF16),
            pltpu.VMEM((SLOTS, SIDE - 1, BLK, BLK), BF16),
            pltpu.VMEM((2, SIDE, SIDE, 8, 128), F32),
            pltpu.VMEM((SIDE, SIDE, 8, 128), F32),
            pltpu.VMEM((2 * SIDE - 2, SIDE, 8, 128), F32),
            pltpu.VMEM((SIDE - 1, SIDE, 8, 128), F32),
            pltpu.VMEM((SIDE - 1, SIDE, 8, 128), F32),
            pltpu.VMEM((2, PH, 128), BF16),
            pltpu.VMEM((2, PH, 128), BF16),
            pltpu.VMEM((2, PH, PH), BF16),
            pltpu.VMEM((2, PH, PH), BF16),
            pltpu.VMEM((PH, PH), BF16),
            pltpu.VMEM((PH, PH), BF16),
            pltpu.VMEM((NBAND, height, PH), F32),
            pltpu.VMEM((2, height // 2, PH), BF16),
            pltpu.VMEM((2, height // 2, PH), BF16),
            pltpu.VMEM((2, 2, height // 2, PH), BF16),
            pltpu.VMEM((2, 2, height // 2, PH), BF16),
            dma((SLOTS, SIDE, SIDE)),
            dma((SLOTS, SIDE - 1, SIDE)),
            dma((SLOTS, SIDE - 1)),
            dma((10,)),
            dma((7,)),
            dma((2,)),
            dma((2,)),
            dma((4,)),
            dma((8,)),
        ],
        compiler_params=pltpu.CompilerParams(
            vmem_limit_bytes=36 << 20, collective_id=0, has_side_effects=True
        ),
        name="reduce_partials",
    )(partial, det_taps, noise_var)


def local(blocks, dest_patch, dest_slot, weights, psf_taps, det_taps, noise_var):
    taps = jnp.pad(psf_taps[0].transpose(1, 0, 2), ((0, 0), (0, 0), (0, 128 - TAPS)))
    partial = match_partials(blocks, dest_patch, dest_slot, weights, taps)
    partial = pltpu.with_memory_space_constraint(partial, pltpu.VMEM)
    image, chi = reduce_partials(partial, det_taps[0], noise_var)
    return image[None], chi


def solution(mesh):
    in_specs = (
        P("band", "patch", None, None),
        P("band", "patch"),
        P("band", "patch"),
        P("band", "patch"),
        P("band", "patch", None, None),
        P("band", None),
        P("band"),
    )
    out_specs = (P("band", None, "patch"), P("band", "patch"))
    return jax.shard_map(local, mesh=mesh, in_specs=in_specs, out_specs=out_specs, check_vma=False)
```

time: 101 us -> 85 us (0.84)
  Pallas kernels: 88.4 us -> 81.1 us
  local copies, waits for them, and re-layouts: 7.73 us -> 2.41 us
  other arithmetic: 2.84 us -> 0 us
    pallas_call x1, Pallas kernels: 78.8 us -> 73.3 us  [reduce_partials(): pl.pallas_call(reduce_kernel, out_shape=(jax.ShapeDtypeStruct((PH, PH), F...]
    unnamed x10 -> x5, local copies, waits for them, and re-layouts: 7.41 us -> 2.4 us
    pallas_call x1, Pallas kernels: 9.63 us -> 7.85 us  [match_partials(): pl.pallas_call(match_kernel, out_shape=pltpu.VMEM((NPATCH * SLOTS + 1, BL...]
    convert_element_type x2 -> x0, other arithmetic: 1.4 us -> none  [the longest x1 0.74 us: local(): taps = psf_taps[0].astype(F32)]
where the time goes in v3:
time: 85 us; the launch traced here: 84.8 us
  Pallas kernels  81.1 us (95%)
  local copies, waits for them, and re-layouts  2.41 us (3%)
  between operations  1.32 us (2%)
    pallas_call x1, Pallas kernels, reduce_partials(): pl.pallas_call(reduce_kernel, out_shape=(jax.ShapeDtypeStruct((PH, PH), F...  73.3 us
    pallas_call x1, Pallas kernels, match_partials(): pl.pallas_call(match_kernel, out_shape=pltpu.VMEM((NPATCH * SLOTS + 1, BL...  7.85 us
    unnamed x5, local copies, waits for them, and re-layouts  2.4 us

profile of v3, /device:TPU:0, one launch (start us, length us, event | category | flops | bytes accessed | tf_op | source)
XLA Modules:
  0.0 84.8 jit_solution(6700918417446053940)
XLA Ops:
  0.6 0.0 copy-start
  1.3 0.7 copy.11
  2.0 7.9 %match_partials.1.d_ref = bf16[129,256,256]{2,1,0:T(8,128)(2,1)S(1)} custom-call(s32[1,32]{1,0:T(1,128)} %patch_hbm.1, s32[1,32]{1,0:T(1,128)} %slot_hbm.1, bf16[1,32]{1,0:T(2,128)(2,1)} %weight_hbm.1, bf16[2,32,128]{2,1,0:T(8,128)(2,1)S(1)} %pad.4.taps_ref, bf16[1,32,256,256]{3,2,1,0:T(8,128)(2,1)} %blocks_hbm.1), custom_call_target="tpu_custom_call" | custom-call | tf_op jit(solution)/shard_map/match_partials/pallas_call | solution.py:103
  9.9 0.0 copy-done
  9.9 73.3 %reduce_partials.1 = (f32[512,512]{1,0:T(8,128)S(1)}, f32[128,512]{1,0:T(8,128)S(1)}) custom-call(bf16[129,256,256]{2,1,0:T(8,128)(2,1)S(1)} %match_partials.1.d_ref, f32[25]{0:T(128)S(1)} %bitcast.8, f32[1]{0:T(128)S(6)} %copy.14.noise_ref), custom_call_target="tpu_custom_call" | custom-call | tf_op jit(solution)/shard_map/reduce_partials/pallas_call | solution.py:394
  83.2 1.0 %copy.15 = f32[1,512,512]{2,1,0:T(8,128)} copy(f32[1,512,512]{2,1,0:T(8,128)S(1)} %bitcast.7) | data formatting | bytes 2097152
  84.1 0.7 copy.16
  (1 shorter events, 0.0 us)
Async XLA Ops:
  0.6 9.3 %copy-start = (f32[1,25]{1,0:T(1,128)S(1)}, f32[1,25]{1,0:T(1,128)}, u32[]{:S(2)}) copy-start(f32[1,25]{1,0:T(1,128)} %param.12) | copy-start | bytes 304

commit v4 on v3

--- a/solution.py
+++ b/solution.py
@@ -38,7 +38,7 @@
 
 def match_kernel(
     patch_hbm, slot_hbm, weight_hbm, taps_ref, blocks_hbm, out_ref,
-    patch_ref, slot_ref, weight_ref, blocks, table_ref, tap_rows, weight_rows, mats, sems, small_sems,
+    patch_ref, slot_ref, weight_ref, blocks, table_ref, tap_rows, weight_rows, even_mats, odd_mats, sems, small_sems,
 ):
     count = blocks.shape[0]
 
@@ -54,24 +54,30 @@
         copy.start()
     for g in range(count // GROUP):
         fetch(g).start()
-    mats[...] = jnp.zeros_like(mats)
+    even_mats[...] = jnp.zeros_like(even_mats)
+    odd_mats[...] = jnp.zeros_like(odd_mats)
     table_ref[...] = jnp.zeros_like(table_ref)
     tap_rows[0] = taps_ref[0].astype(F32)
     ends = lax.broadcasted_iota(jnp.int32, (128, 128), 0) + lax.broadcasted_iota(jnp.int32, (128, 128), 1)
     reverse = jnp.where(ends == TAPS - 1, 1.0, 0.0).astype(BF16)
     tap_rows[1] = jnp.dot(taps_ref[1], reverse, preferred_element_type=F32)
+    groups = count // GROUP
+
+    def build(g, mats):
+        for n in range(GROUP):
+            for axis in range(2):
+                toeplitz_store(tap_rows[axis, pl.ds(g * GROUP + n, 1), :], mats.at[n, axis])
+
+    build(0, even_mats)
     for copy in small:
         copy.wait()
     diagonal = lax.broadcasted_iota(jnp.int32, (count, count), 0) == lax.broadcasted_iota(jnp.int32, (count, count), 1)
     spread = jnp.where(diagonal, jnp.broadcast_to(weight_ref[...].astype(F32), (count, count)), 0.0)
     weight_rows[...] = jnp.broadcast_to(jnp.sum(spread, axis=1, keepdims=True), (count, 128))
 
-    @pl.loop(0, count // GROUP)
-    def _(g):
+    def match(g, mats, later):
         fetch(g).wait()
-        for n in range(GROUP):
-            for axis in range(2):
-                toeplitz_store(tap_rows[axis, pl.ds(g * GROUP + n, 1), :], mats.at[n, axis])
+        build(lax.min(g + 1, groups - 1), later)
         halves = []
         for n in range(GROUP):
             half = jnp.dot(mats[n, 0], blocks[g * GROUP + n], preferred_element_type=F32)
@@ -89,6 +95,11 @@
             tile = patch * SLOTS + slot
             old = jnp.where(wide(before) > 0.0, out_ref[tile].astype(F32), 0.0)
             out_ref[tile] = (old + wide(weight) * full.astype(F32)).astype(BF16)
+
+    @pl.loop(0, groups // 2)
+    def _(pair):
+        match(2 * pair, even_mats, odd_mats)
+        match(2 * pair + 1, odd_mats, even_mats)
 
     high, low = split(table_ref[...].reshape(NPATCH * 8, 128))
     out_ref[NPATCH * SLOTS, :, 0:128] = high
@@ -114,6 +125,7 @@
             pltpu.VMEM((2, count, 128), F32),
             pltpu.VMEM((count, 128), F32),
             pltpu.VMEM((GROUP, 2, BLK, BLK), BF16),
+            pltpu.VMEM((GROUP, 2, BLK, BLK), BF16),
             pltpu.SemaphoreType.DMA((count // GROUP,)),
             pltpu.SemaphoreType.DMA((3,)),
         ],
@@ -152,14 +164,17 @@
 def build_tables(det_ref, col_tab, row_tab):
     col_tab[...] = jnp.zeros_like(col_tab)
     row_tab[...] = jnp.zeros_like(row_tab)
-    for table, sign in ((row_tab, 1), (col_tab, -1)):
+    for sign in (1, -1):
         for diag in (-1, 0, 1):
             high, low = split(tap_block(det_ref, sign * 128 * diag, sign))
             for rb in range(PH // 128):
                 cb = rb + diag
                 if 0 <= cb < PH // 128:
-                    table[0, 128 * rb : 128 * rb + 128, 128 * cb : 128 * cb + 128] = high
-                    table[1, 128 * rb : 128 * rb + 128, 128 * cb : 128 * cb + 128] = low
+                    for n, part in enumerate((high, low)):
+                        if sign == 1:
+                            row_tab[n, rb, :, 128 * cb : 128 * cb + 128] = part
+                        else:
+                            col_tab[n, 128 * rb : 128 * rb + 128, 128 * cb : 128 * cb + 128] = part
 
 
 def reduce_kernel(
@@ -229,11 +244,13 @@
     w_exchange = remote(w_ref.at[1 - core], w_pair, send_sem.at[3], w_sem.at[0], partner)
     w_exchange.start()
 
-    @pl.loop(0, SIDE)
-    def _(k):
-        for s in range(SLOTS):
-            send_pair(s, 0, k)
-
+    def send_pairs(h, first):
+        @pl.loop(first, first + 2)
+        def _(k):
+            for s in range(SLOTS):
+                send_pair(s, h, k)
+
+    send_pairs(0, 0)
     w_exchange.wait_recv()
 
     def w_here(h):
@@ -255,25 +272,23 @@
         other = jnp.where(wide(w_pair[z, y, s : s + 1]) > 0.0, pair[s, h, k].astype(F32), 0.0)
         return mine + other
 
-    w_acc[0] = w_here(0)
-    w_copy1(0).start()
-
-    @pl.loop(0, SIDE)
-    def _(k):
-        for s in range(SLOTS):
-            wait_pair(s, 0, k)
-            pair[s, 0, k] = here(s, 0, k).astype(BF16)
-            hop1_copy(s, 0, k).start()
-            send_pair(s, 1, k)
-
-    build_tables(det_ref, col_tab, row_tab)
-
-    @pl.loop(1, SIDE - 1)
-    def _(h):
-        @pl.loop(0, SIDE)
+    def start_units(first, *ahead):
+        @pl.loop(first, first + 2)
         def _(k):
+            for later, start in ahead:
+                for s in range(SLOTS):
+                    send_pair(s, later, k - first + start)
             for s in range(SLOTS):
-                send_pair(s, h + 1, k)
+                wait_pair(s, 0, k)
+                pair[s, 0, k] = here(s, 0, k).astype(BF16)
+                hop1_copy(s, 0, k).start()
+
+    def pass_units(h, first, *ahead):
+        @pl.loop(first, first + 2)
+        def _(k):
+            for later, start in ahead:
+                for s in range(SLOTS):
+                    send_pair(s, later, k - first + start)
             for s in range(SLOTS):
                 wait_pair(s, h, k)
                 total = here(s, h, k)
@@ -281,95 +296,124 @@
                 pair[s, h, k] = (total + hop1[s, h - 1, k].astype(F32)).astype(BF16)
                 hop1_copy(s, h, k).start()
 
-        w_copy1(h - 1).wait_recv()
-        w_acc[h] = w_here(h) + w_hop1[h - 1]
-        w_copy1(h).start()
-
     def gathered(s, k):
         wait_pair(s, 3, k)
         hop1_copy(s, 2, k).wait_recv()
         return here(s, 3, k) + hop1[s, 2, k].astype(F32)
 
-    for s in range(SLOTS):
-        pair[s, 3, 0] = gathered(s, 0).astype(BF16)
-        hop2_copy(s, 0).start()
-
-    w_copy1(2).wait_recv()
-    w_acc[3] = w_here(3) + w_hop1[2]
-    w_copy2(0).start()
-
-    @pl.loop(1, SIDE - 1)
-    def _(k):
+    def turn_units(k):
         for s in range(SLOTS):
             total = gathered(s, k)
-            hop2_copy(s, k - 1).wait_recv()
-            pair[s, 3, k] = (total + hop2[s, k - 1].astype(F32)).astype(BF16)
+            if k > 0:
+                hop2_copy(s, k - 1).wait_recv()
+                total = total + hop2[s, k - 1].astype(F32)
+            pair[s, 3, k] = total.astype(BF16)
             hop2_copy(s, k).start()
-        w_copy2(k - 1).wait_recv()
-        w_acc[3 + k] = w_acc[3] + w_hop2[k - 1]
-        w_copy2(k).start()
-
+
+    def w_step(n):
+        if n > 0:
+            (w_copy1(n - 1) if n < 4 else w_copy2(n - 4)).wait_recv()
+        if n < 3:
+            w_acc[n] = w_here(n) + w_hop1[n - 1] if n > 0 else w_here(n)
+            w_copy1(n).start()
+        else:
+            w_acc[n] = w_here(3) + w_hop1[2] if n == 3 else w_acc[3] + w_hop2[n - 4]
+            w_copy2(n - 3).start()
+
+    w_step(0)
+    start_units(0, (1, 0))
+    build_tables(det_ref, col_tab, row_tab)
+    pass_units(1, 0, (2, 0))
+    w_step(1)
+    pass_units(2, 0, (0, 2))
+    w_step(2)
+    start_units(2, (3, 0), (1, 2))
+    w_step(3)
+    turn_units(0)
+    pass_units(1, 2, (2, 2))
+    w_step(4)
+    turn_units(1)
+    pass_units(2, 2, (3, 2))
+    w_step(5)
+    turn_units(2)
     w_copy2(2).wait_recv()
     weight_sum = w_acc[3, place[0]] + w_hop2[2, place[0]]
-    scale = jnp.maximum(weight_sum, 1.0)
-
-    for s in range(SLOTS):
-        total = gathered(s, 3)
-        hop2_copy(s, 2).wait_recv()
-        total = total + hop2[s, 2].astype(F32)
-        divisor = jnp.broadcast_to(scale[s : s + 1, 0:1], (BLK, BLK))
-        value = total / divisor
-        rows = slice((s // 2) * BLK, (s // 2 + 1) * BLK)
-        cols = slice((s % 2) * BLK, (s % 2 + 1) * BLK)
-        img_ref[rows, cols] = value
-        high[rows, cols], low[rows, cols] = split(value)
-
-    halo_out[0] = high[:, 0:128]
-    halo_out[1] = high[:, PH - 128 : PH]
-    to_before = remote(halo_out.at[0], halo_in.at[1], end_sem.at[0], halo_sem.at[1], before)
-    to_after = remote(halo_out.at[1], halo_in.at[0], end_sem.at[1], halo_sem.at[0], after)
-    to_before.start()
-    to_after.start()
+    scale = 1.0 / jnp.maximum(weight_sum, 1.0)
+
+    def halo_copy(d, half):
+        rows = pl.ds(half * BLK, BLK)
+        device = after if d == 0 else before
+        return remote(
+            halo_out.at[d, rows], halo_in.at[d, rows], end_sem.at[2 * half + d], halo_sem.at[2 * half + d], device
+        )
+
+    for half in range(2):
+        rows = slice(half * BLK, (half + 1) * BLK)
+        for s in (2 * half, 2 * half + 1):
+            total = gathered(s, 3)
+            hop2_copy(s, 2).wait_recv()
+            value = (total + hop2[s, 2].astype(F32)) * jnp.broadcast_to(scale[s : s + 1, 0:1], (BLK, BLK))
+            cols = slice((s % 2) * BLK, (s % 2 + 1) * BLK)
+            img_ref[rows, cols] = value
+            high[rows, cols], low[rows, cols] = split(value)
+        halo_out[0, rows] = high[rows, PH - 128 : PH]
+        halo_out[1, rows] = high[rows, 0:128]
+        for d in range(2):
+            halo_copy(d, half).start()
+
     high[...], low[...] = split(dot3(high[...], low[...], col_tab[0], col_tab[1]))
-    row = dot3(row_tab[0], row_tab[1], high[...], low[...])
-    to_before.wait_recv()
-    to_after.wait_recv()
+    for half in range(2):
+        for d in range(2):
+            halo_copy(d, half).wait_recv()
     dot = lambda a, b: jnp.dot(a, b, preferred_element_type=F32)
     left = halo_in[0]
     right = halo_in[1]
     from_left = dot(left, col_tab[0, 0:128, 128:256]) + dot(left, col_tab[1, 0:128, 128:256])
     from_right = dot(right, col_tab[0, 128:256, 0:128]) + dot(right, col_tab[1, 128:256, 0:128])
     edge_high, edge_low = split(jnp.concatenate([from_left, from_right], axis=1))
-    edge = dot3(row_tab[0], row_tab[1], edge_high, edge_low)
-    row = jnp.concatenate(
-        [row[:, 0:128] + edge[:, 0:128], row[:, 128 : PH - 128], row[:, PH - 128 : PH] + edge[:, 128:256]],
-        axis=1,
-    )
-    squares = row * row / noise_ref[0]
     height = PH // NBAND
     part = height // 2
-    for g in range(NBAND):
-        term[g] = squares[g * height : (g + 1) * height]
     opposite = lax.rem(band + 2, NBAND)
     near = (above, below)
-    far_copy = lambda d: remote(far_out.at[d], far_in.at[d], end_sem.at[2 + d], far_sem.at[d], near[d], "band")
+    over_noise = (1.0 / jnp.full((8, 128), noise_ref[0], F32))[0:1, 0:1]
+
+    def rows_of(first, chunks):
+        row_high = jnp.concatenate([row_tab[0, g] for g in chunks], axis=0)
+        row_low = jnp.concatenate([row_tab[1, g] for g in chunks], axis=0)
+        row = dot3(row_high, row_low, high[...], low[...])
+        edge = dot3(row_high, row_low, edge_high, edge_low)
+        row = jnp.concatenate(
+            [row[:, 0:128] + edge[:, 0:128], row[:, 128 : PH - 128], row[:, PH - 128 : PH] + edge[:, 128:256]],
+            axis=1,
+        )
+        squares = row * row * jnp.broadcast_to(over_noise, row.shape)
+        for n in range(len(chunks)):
+            term[first + n] = squares[n * height : (n + 1) * height]
+
+    far_copy = lambda d: remote(far_out.at[d], far_in.at[d], end_sem.at[4 + d], far_sem.at[d], near[d], "band")
     near_copy = lambda d, n: remote(
-        near_out.at[d, n], near_in.at[d, n], end_sem.at[4 + 2 * d + n], near_sem.at[2 * d + n], near[d], "band"
+        near_out.at[d, n], near_in.at[d, n], end_sem.at[6 + 2 * d + n], near_sem.at[2 * d + n], near[d], "band"
     )
+
+    def send_early(d):
+        near_out[d, 1 - d] = term[1 + d, (1 - d) * part : (2 - d) * part].astype(BF16)
+        near_copy(d, 1 - d).start()
+
+    rows_of(0, (opposite, above))
     for d in range(2):
-        far_out[d] = term[opposite, d * part : (d + 1) * part].astype(BF16)
+        far_out[d] = term[0, d * part : (d + 1) * part].astype(BF16)
         far_copy(d).start()
-    for d in range(2):
-        near_out[d, 1 - d] = term[near[d], (1 - d) * part : (2 - d) * part].astype(BF16)
-        near_copy(d, 1 - d).start()
+    send_early(0)
+    rows_of(2, (below, band))
+    send_early(1)
     for d in range(2):
         far_copy(d).wait_recv()
-        near_out[d, d] = (term[near[d], d * part : (d + 1) * part] + far_in[d].astype(F32)).astype(BF16)
+        near_out[d, d] = (term[1 + d, d * part : (d + 1) * part] + far_in[d].astype(F32)).astype(BF16)
         near_copy(d, d).start()
     for n in range(2):
         near_copy(0, n).wait_recv()
         near_copy(1, n).wait_recv()
-        own = term[band, n * part : (n + 1) * part]
+        own = term[3, n * part : (n + 1) * part]
         chi_ref[n * part : (n + 1) * part] = own + (near_in[0, n].astype(F32) + near_in[1, n].astype(F32))
 
     for index, ref in enumerate((pair, hop1, hop2)):
@@ -378,8 +422,9 @@
     for h in range(SIDE - 1):
         w_copy1(h).wait_send()
         w_copy2(h).wait_send()
-    to_before.wait_send()
-    to_after.wait_send()
+    for half in range(2):
+        for d in range(2):
+            halo_copy(d, half).wait_send()
     for d in range(2):
         far_copy(d).wait_send()
         for n in range(2):
@@ -411,7 +456,7 @@
             pltpu.VMEM((2, PH, 128), BF16),
             pltpu.VMEM((2, PH, 128), BF16),
             pltpu.VMEM((2, PH, PH), BF16),
-            pltpu.VMEM((2, PH, PH), BF16),
+            pltpu.VMEM((2, PH // 128, 128, PH), BF16),
             pltpu.VMEM((PH, PH), BF16),
             pltpu.VMEM((PH, PH), BF16),
             pltpu.VMEM((NBAND, height, PH), F32),
@@ -424,10 +469,10 @@
             dma((SLOTS, SIDE - 1)),
             dma((10,)),
             dma((7,)),
-            dma((2,)),
+            dma((4,)),
             dma((2,)),
             dma((4,)),
-            dma((8,)),
+            dma((10,)),
         ],
         compiler_params=pltpu.CompilerParams(
             vmem_limit_bytes=36 << 20, collective_id=0, has_side_effects=True

time: 85 us -> 78.8 us (0.927)
  Pallas kernels: 81.1 us -> 74.9 us
    pallas_call x1, Pallas kernels: 73.3 us -> 68.8 us  [reduce_partials(): pl.pallas_call(reduce_kernel, out_shape=(jax.ShapeDtypeStruct((PH, PH), F...]
    pallas_call x1, Pallas kernels: 7.85 us -> 6.09 us  [match_partials(): pl.pallas_call(match_kernel, out_shape=pltpu.VMEM((NPATCH * SLOTS + 1, BL...]
where the time goes in v4:
time: 78.8 us; the launch traced here: 78.6 us
  Pallas kernels  74.9 us (95%)
  local copies, waits for them, and re-layouts  2.41 us (3%)
  between operations  1.32 us (2%)
    pallas_call x1, Pallas kernels, reduce_partials(): pl.pallas_call(reduce_kernel, out_shape=(jax.ShapeDtypeStruct((PH, PH), F...  68.8 us
    pallas_call x1, Pallas kernels, match_partials(): pl.pallas_call(match_kernel, out_shape=pltpu.VMEM((NPATCH * SLOTS + 1, BL...  6.09 us
    unnamed x5, local copies, waits for them, and re-layouts  2.4 us

profile of v4, /device:TPU:0, one launch (start us, length us, event | category | flops | bytes accessed | tf_op | source)
XLA Modules:
  0.0 78.6 jit_solution(18089351906728266899)
XLA Ops:
  0.6 0.0 copy-start
  1.3 0.7 copy.11
  2.0 6.1 %match_partials.1.d_ref = bf16[129,256,256]{2,1,0:T(8,128)(2,1)S(1)} custom-call(s32[1,32]{1,0:T(1,128)} %patch_hbm.1, s32[1,32]{1,0:T(1,128)} %slot_hbm.1, bf16[1,32]{1,0:T(2,128)(2,1)} %weight_hbm.1, bf16[2,32,128]{2,1,0:T(8,128)(2,1)S(1)} %pad.4.taps_ref, bf16[1,32,256,256]{3,2,1,0:T(8,128)(2,1)} %blocks_hbm.1), custom_call_target="tpu_custom_call" | custom-call | tf_op jit(solution)/shard_map/match_partials/pallas_call | solution.py:114
  8.1 0.0 copy-done
  8.1 68.8 %reduce_partials.1 = (f32[512,512]{1,0:T(8,128)S(1)}, f32[128,512]{1,0:T(8,128)S(1)}) custom-call(bf16[129,256,256]{2,1,0:T(8,128)(2,1)S(1)} %match_partials.1.d_ref, f32[25]{0:T(128)S(1)} %bitcast.8, f32[1]{0:T(128)S(6)} %copy.14.noise_ref), custom_call_target="tpu_custom_call" | custom-call | tf_op jit(solution)/shard_map/reduce_partials/pallas_call | solution.py:439
  76.9 1.0 %copy.15 = f32[1,512,512]{2,1,0:T(8,128)} copy(f32[1,512,512]{2,1,0:T(8,128)S(1)} %bitcast.7) | data formatting | bytes 2097152
  77.9 0.7 copy.16
  (1 shorter events, 0.0 us)
Async XLA Ops:
  0.6 7.5 %copy-start = (f32[1,25]{1,0:T(1,128)S(1)}, f32[1,25]{1,0:T(1,128)}, u32[]{:S(2)}) copy-start(f32[1,25]{1,0:T(1,128)} %param.12) | copy-start | bytes 304

commit v5 on v4

--- a/solution.py
+++ b/solution.py
@@ -10,6 +10,7 @@
 SLOTS = 4
 TAPS = 41
 BLK = 256
+HALF = 128
 PH = 512
 NPATCH = 32
 NBAND = 4
@@ -37,8 +38,8 @@
 
 
 def match_kernel(
-    patch_hbm, slot_hbm, weight_hbm, taps_ref, blocks_hbm, out_ref,
-    patch_ref, slot_ref, weight_ref, blocks, table_ref, tap_rows, weight_rows, even_mats, odd_mats, sems, small_sems,
+    patch_hbm, slot_hbm, weight_hbm, taps_hbm, blocks_hbm, out_ref,
+    patch_ref, slot_ref, weight_ref, taps_ref, blocks, table_ref, tap_rows, weight_rows, even_mats, odd_mats, sems, small_sems,
 ):
     count = blocks.shape[0]
 
@@ -48,7 +49,9 @@
 
     small = [
         pltpu.make_async_copy(src, dst, small_sems.at[n])
-        for n, (src, dst) in enumerate(((weight_hbm, weight_ref), (patch_hbm, patch_ref), (slot_hbm, slot_ref)))
+        for n, (src, dst) in enumerate(
+            ((taps_hbm, taps_ref), (weight_hbm, weight_ref), (patch_hbm, patch_ref), (slot_hbm, slot_ref))
+        )
     ]
     for copy in small:
         copy.start()
@@ -57,19 +60,21 @@
     even_mats[...] = jnp.zeros_like(even_mats)
     odd_mats[...] = jnp.zeros_like(odd_mats)
     table_ref[...] = jnp.zeros_like(table_ref)
-    tap_rows[0] = taps_ref[0].astype(F32)
-    ends = lax.broadcasted_iota(jnp.int32, (128, 128), 0) + lax.broadcasted_iota(jnp.int32, (128, 128), 1)
-    reverse = jnp.where(ends == TAPS - 1, 1.0, 0.0).astype(BF16)
-    tap_rows[1] = jnp.dot(taps_ref[1], reverse, preferred_element_type=F32)
+    small[0].wait()
+    raw = taps_ref[0].astype(F32).reshape(2 * count, TAPS).astype(BF16)
+    from_tap = lax.broadcasted_iota(jnp.int32, (TAPS, 128), 0)
+    to_lane = lax.broadcasted_iota(jnp.int32, (TAPS, 128), 1)
+    for axis, picks in enumerate((from_tap == to_lane, from_tap + to_lane == TAPS - 1)):
+        tap_rows[axis] = jnp.dot(raw, jnp.where(picks, 1.0, 0.0).astype(BF16), preferred_element_type=F32)
     groups = count // GROUP
 
     def build(g, mats):
         for n in range(GROUP):
             for axis in range(2):
-                toeplitz_store(tap_rows[axis, pl.ds(g * GROUP + n, 1), :], mats.at[n, axis])
+                toeplitz_store(tap_rows[axis, pl.ds(2 * (g * GROUP + n) + axis, 1), :], mats.at[n, axis])
 
     build(0, even_mats)
-    for copy in small:
+    for copy in small[1:]:
         copy.wait()
     diagonal = lax.broadcasted_iota(jnp.int32, (count, count), 0) == lax.broadcasted_iota(jnp.int32, (count, count), 1)
     spread = jnp.where(diagonal, jnp.broadcast_to(weight_ref[...].astype(F32), (count, count)), 0.0)
@@ -114,24 +119,25 @@
     return pl.pallas_call(
         match_kernel,
         out_shape=pltpu.VMEM((NPATCH * SLOTS + 1, BLK, BLK), BF16),
-        in_specs=[hbm, hbm, hbm, vmem, hbm],
+        in_specs=[hbm] * 5,
         out_specs=vmem,
         scratch_shapes=[
             pltpu.SMEM((1, count), jnp.int32),
             pltpu.SMEM((1, count), jnp.int32),
             pltpu.VMEM((1, count), BF16),
+            pltpu.VMEM(taps.shape, BF16),
             pltpu.VMEM((count, BLK, BLK), BF16),
             pltpu.VMEM((NPATCH, 8, 128), F32),
-            pltpu.VMEM((2, count, 128), F32),
+            pltpu.VMEM((2, 2 * count, 128), F32),
             pltpu.VMEM((count, 128), F32),
             pltpu.VMEM((GROUP, 2, BLK, BLK), BF16),
             pltpu.VMEM((GROUP, 2, BLK, BLK), BF16),
             pltpu.SemaphoreType.DMA((count // GROUP,)),
-            pltpu.SemaphoreType.DMA((3,)),
+            pltpu.SemaphoreType.DMA((4,)),
         ],
         compiler_params=pltpu.CompilerParams(vmem_limit_bytes=28 << 20),
         name="match_partials",
-    )(keep(dest_patch), keep(dest_slot), keep(weights), taps, keep(blocks))
+    )(*(keep(x) for x in (dest_patch, dest_slot, weights, taps, blocks)))
 
 
 def wrap(x):
@@ -235,8 +241,11 @@
     def hop1_copy(s, h, k):
         return remote(pair.at[s, h, k], hop1.at[s, h, k], send_sem.at[1], hop1_sem.at[s, h, k], next1[s])
 
-    def hop2_copy(s, k):
-        return remote(pair.at[s, 3, k], hop2.at[s, k], send_sem.at[2], hop2_sem.at[s, k], next2[s])
+    def hop2_copy(s, k, sub):
+        rows = pl.ds(sub * HALF, HALF)
+        return remote(
+            pair.at[s, 3, k, rows], hop2.at[s, k, rows], send_sem.at[2], hop2_sem.at[s, k, sub], next2[s]
+        )
 
     table = d_ref[NPATCH * SLOTS]
     table = table[:, 0:128].astype(F32) + table[:, 128:256].astype(F32)
@@ -263,13 +272,14 @@
     def w_copy2(k):
         return remote(w_acc.at[3 + k], w_hop2.at[k], send_sem.at[7 + k], w_sem.at[4 + k], moved(0, 1))
 
-    def here(s, h, k):
+    def here(s, h, k, rows=slice(0, BLK)):
         y, z = dest(s, h, k)
-        wide = lambda row: jnp.broadcast_to(jnp.concatenate([row, row], axis=1), (BLK, BLK))
+        height = rows.stop - rows.start
+        wide = lambda row: jnp.broadcast_to(jnp.concatenate([row, row], axis=1), (height, BLK))
         mine = jnp.where(
-            wide(w_ref[core, z, y, s : s + 1]) > 0.0, d_ref[tile(s, h, k, core)].astype(F32), 0.0
+            wide(w_ref[core, z, y, s : s + 1]) > 0.0, d_ref[tile(s, h, k, core), rows].astype(F32), 0.0
         )
-        other = jnp.where(wide(w_pair[z, y, s : s + 1]) > 0.0, pair[s, h, k].astype(F32), 0.0)
+        other = jnp.where(wide(w_pair[z, y, s : s + 1]) > 0.0, pair[s, h, k, rows].astype(F32), 0.0)
         return mine + other
 
     def start_units(first, *ahead):
@@ -296,19 +306,22 @@
                 pair[s, h, k] = (total + hop1[s, h - 1, k].astype(F32)).astype(BF16)
                 hop1_copy(s, h, k).start()
 
-    def gathered(s, k):
-        wait_pair(s, 3, k)
-        hop1_copy(s, 2, k).wait_recv()
-        return here(s, 3, k) + hop1[s, 2, k].astype(F32)
+    def gathered(s, k, sub):
+        rows = slice(sub * HALF, (sub + 1) * HALF)
+        if sub == 0:
+            wait_pair(s, 3, k)
+            hop1_copy(s, 2, k).wait_recv()
+        total = here(s, 3, k, rows) + hop1[s, 2, k, rows].astype(F32)
+        if k > 0:
+            hop2_copy(s, k - 1, sub).wait_recv()
+            total = total + hop2[s, k - 1, rows].astype(F32)
+        return total
 
     def turn_units(k):
-        for s in range(SLOTS):
-            total = gathered(s, k)
-            if k > 0:
-                hop2_copy(s, k - 1).wait_recv()
-                total = total + hop2[s, k - 1].astype(F32)
-            pair[s, 3, k] = total.astype(BF16)
-            hop2_copy(s, k).start()
+        for sub in range(2):
+            for s in range(SLOTS):
+                pair[s, 3, k, sub * HALF : (sub + 1) * HALF] = gathered(s, k, sub).astype(BF16)
+                hop2_copy(s, k, sub).start()
 
     def w_step(n):
         if n > 0:
@@ -340,34 +353,35 @@
     weight_sum = w_acc[3, place[0]] + w_hop2[2, place[0]]
     scale = 1.0 / jnp.maximum(weight_sum, 1.0)
 
-    def halo_copy(d, half):
-        rows = pl.ds(half * BLK, BLK)
+    def halo_copy(d, sub):
         device = after if d == 0 else before
         return remote(
-            halo_out.at[d, rows], halo_in.at[d, rows], end_sem.at[2 * half + d], halo_sem.at[2 * half + d], device
+            halo_out.at[d, sub], halo_in.at[d, sub], end_sem.at[2 * sub + d], halo_sem.at[2 * sub + d], device
         )
 
-    for half in range(2):
-        rows = slice(half * BLK, (half + 1) * BLK)
-        for s in (2 * half, 2 * half + 1):
-            total = gathered(s, 3)
-            hop2_copy(s, 2).wait_recv()
-            value = (total + hop2[s, 2].astype(F32)) * jnp.broadcast_to(scale[s : s + 1, 0:1], (BLK, BLK))
+    for sub in range(2):
+        for s in range(SLOTS):
+            value = gathered(s, 3, sub) * jnp.broadcast_to(scale[s : s + 1, 0:1], (HALF, BLK))
+            top = (s // 2) * BLK + sub * HALF
+            rows = slice(top, top + HALF)
             cols = slice((s % 2) * BLK, (s % 2 + 1) * BLK)
             img_ref[rows, cols] = value
             high[rows, cols], low[rows, cols] = split(value)
-        halo_out[0, rows] = high[rows, PH - 128 : PH]
-        halo_out[1, rows] = high[rows, 0:128]
+        for half in range(2):
+            top = half * BLK + sub * HALF
+            rows = slice(top, top + HALF)
+            halo_out[0, sub, half] = high[rows, PH - 128 : PH]
+            halo_out[1, sub, half] = high[rows, 0:128]
         for d in range(2):
-            halo_copy(d, half).start()
+            halo_copy(d, sub).start()
 
     high[...], low[...] = split(dot3(high[...], low[...], col_tab[0], col_tab[1]))
-    for half in range(2):
+    for sub in range(2):
         for d in range(2):
-            halo_copy(d, half).wait_recv()
+            halo_copy(d, sub).wait_recv()
     dot = lambda a, b: jnp.dot(a, b, preferred_element_type=F32)
-    left = halo_in[0]
-    right = halo_in[1]
+    sides = [jnp.concatenate([halo_in[d, n % 2, n // 2] for n in range(4)], axis=0) for d in range(2)]
+    left, right = sides
     from_left = dot(left, col_tab[0, 0:128, 128:256]) + dot(left, col_tab[1, 0:128, 128:256])
     from_right = dot(right, col_tab[0, 128:256, 0:128]) + dot(right, col_tab[1, 128:256, 0:128])
     edge_high, edge_low = split(jnp.concatenate([from_left, from_right], axis=1))
@@ -422,9 +436,9 @@
     for h in range(SIDE - 1):
         w_copy1(h).wait_send()
         w_copy2(h).wait_send()
-    for half in range(2):
+    for sub in range(2):
         for d in range(2):
-            halo_copy(d, half).wait_send()
+            halo_copy(d, sub).wait_send()
     for d in range(2):
         far_copy(d).wait_send()
         for n in range(2):
@@ -453,8 +467,8 @@
             pltpu.VMEM((2 * SIDE - 2, SIDE, 8, 128), F32),
             pltpu.VMEM((SIDE - 1, SIDE, 8, 128), F32),
             pltpu.VMEM((SIDE - 1, SIDE, 8, 128), F32),
-            pltpu.VMEM((2, PH, 128), BF16),
-            pltpu.VMEM((2, PH, 128), BF16),
+            pltpu.VMEM((2, 2, 2, HALF, 128), BF16),
+            pltpu.VMEM((2, 2, 2, HALF, 128), BF16),
             pltpu.VMEM((2, PH, PH), BF16),
             pltpu.VMEM((2, PH // 128, 128, PH), BF16),
             pltpu.VMEM((PH, PH), BF16),
@@ -466,7 +480,7 @@
             pltpu.VMEM((2, 2, height // 2, PH), BF16),
             dma((SLOTS, SIDE, SIDE)),
             dma((SLOTS, SIDE - 1, SIDE)),
-            dma((SLOTS, SIDE - 1)),
+            dma((SLOTS, SIDE - 1, 2)),
             dma((10,)),
             dma((7,)),
             dma((4,)),
@@ -481,11 +495,34 @@
     )(partial, det_taps, noise_var)
 
 
+def write_kernel(image, chi, image_hbm, chi_hbm, sems):
+    copies = [
+        pltpu.make_async_copy(src, dst, sems.at[n]) for n, (src, dst) in enumerate(((image, image_hbm), (chi, chi_hbm)))
+    ]
+    for copy in copies:
+        copy.start()
+    for copy in copies:
+        copy.wait()
+
+
+def write_out(image, chi):
+    hbm = pl.BlockSpec(memory_space=pltpu.HBM)
+    vmem = pl.BlockSpec(memory_space=pltpu.VMEM)
+    return pl.pallas_call(
+        write_kernel,
+        out_shape=tuple(jax.ShapeDtypeStruct(x.shape, x.dtype) for x in (image, chi)),
+        in_specs=[vmem, vmem],
+        out_specs=(hbm, hbm),
+        scratch_shapes=[pltpu.SemaphoreType.DMA((2,))],
+        name="write_out",
+    )(*(pltpu.with_memory_space_constraint(x, pltpu.VMEM) for x in (image, chi)))
+
+
 def local(blocks, dest_patch, dest_slot, weights, psf_taps, det_taps, noise_var):
-    taps = jnp.pad(psf_taps[0].transpose(1, 0, 2), ((0, 0), (0, 0), (0, 128 - TAPS)))
-    partial = match_partials(blocks, dest_patch, dest_slot, weights, taps)
+    partial = match_partials(blocks, dest_patch, dest_slot, weights, psf_taps)
     partial = pltpu.with_memory_space_constraint(partial, pltpu.VMEM)
     image, chi = reduce_partials(partial, det_taps[0], noise_var)
+    image, chi = write_out(image, chi)
     return image[None], chi
 
 

time: 78.8 us -> 77.1 us (0.978)
  local copies, waits for them, and re-layouts: 2.41 us -> 0.01 us
  Pallas kernels: 74.9 us -> 75.7 us
    unnamed x5 -> x2, local copies, waits for them, and re-layouts: 2.4 us -> 0.01 us
    pallas_call x0 -> x1, Pallas kernels: none -> 1.07 us  [write_out(): pl.pallas_call(write_kernel, out_shape=tuple((jax.ShapeDtypeStruct(x.shap...]
where the time goes in v5:
time: 77.1 us; the launch traced here: 77 us
  Pallas kernels  75.7 us (98%)
  between operations  1.32 us (2%)
    pallas_call x1, Pallas kernels, reduce_partials(): pl.pallas_call(reduce_kernel, out_shape=(jax.ShapeDtypeStruct((PH, PH), F...  68.1 us
    pallas_call x1, Pallas kernels, match_partials(): pl.pallas_call(match_kernel, out_shape=pltpu.VMEM((NPATCH * SLOTS + 1, BL...  6.53 us

profile of v5, /device:TPU:0, one launch (start us, length us, event | category | flops | bytes accessed | tf_op | source)
XLA Modules:
  0.0 77.0 jit_solution(4554858281539877460)
XLA Ops:
  0.6 0.0 copy-start
  1.3 6.5 %match_partials.1.d_ref = bf16[129,256,256]{2,1,0:T(8,128)(2,1)S(1)} custom-call(s32[1,32]{1,0:T(1,128)} %patch_hbm.1, s32[1,32]{1,0:T(1,128)} %slot_hbm.1, bf16[1,32]{1,0:T(2,128)(2,1)} %weight_hbm.1, bf16[1,32,2,41]{3,2,1,0:T(2,128)(2,1)} %taps_hbm.1, bf16[1,32,256,256]{3,2,1,0:T(8,128)(2,1)} %blocks_hbm.1), custom_call_target="tpu_custom_call" | custom-call | tf_op jit(solution)/shard_map/match_partials/pallas_call | solution.py:119
  7.8 0.0 copy-done
  7.9 68.1 %reduce_partials.1 = (f32[512,512]{1,0:T(8,128)S(1)}, f32[128,512]{1,0:T(8,128)S(1)}) custom-call(bf16[129,256,256]{2,1,0:T(8,128)(2,1)S(1)} %match_partials.1.d_ref, f32[25]{0:T(128)S(1)} %bitcast.2, f32[1]{0:T(128)S(6)} %copy.9.noise_ref), custom_call_target="tpu_custom_call" | custom-call | tf_op jit(solution)/shard_map/reduce_partials/pallas_call | solution.py:453
  76.0 1.1 %write_out.1 = (f32[512,512]{1,0:T(8,128)}, f32[128,512]{1,0:T(8,128)}) custom-call(f32[512,512]{1,0:T(8,128)S(1)} %get-tuple-element.6.image, f32[128,512]{1,0:T(8,128)S(1)} %get-tuple-element.7.chi), custom_call_target="tpu_custom_call" | custom-call | tf_op jit(solution)/shard_map/write_out/pallas_call | solution.py:511
Async XLA Ops:
  0.6 7.2 %copy-start = (f32[1,25]{1,0:T(1,128)S(1)}, f32[1,25]{1,0:T(1,128)}, u32[]{:S(2)}) copy-start(f32[1,25]{1,0:T(1,128)} %param.12) | copy-start | bytes 304

commit v6 on v5

--- a/solution.py
+++ b/solution.py
@@ -11,6 +11,7 @@
 TAPS = 41
 BLK = 256
 HALF = 128
+EDGE = 16
 PH = 512
 NPATCH = 32
 NBAND = 4
@@ -359,6 +360,9 @@
             halo_out.at[d, sub], halo_in.at[d, sub], end_sem.at[2 * sub + d], halo_sem.at[2 * sub + d], device
         )
 
+    lane = lax.broadcasted_iota(jnp.int32, (EDGE, 128), 1) - lax.broadcasted_iota(jnp.int32, (EDGE, 128), 0)
+    pick = [jnp.where(lane == first, 1.0, 0.0).astype(BF16) for first in (128 - EDGE, 0)]
+
     for sub in range(2):
         for s in range(SLOTS):
             value = gathered(s, 3, sub) * jnp.broadcast_to(scale[s : s + 1, 0:1], (HALF, BLK))
@@ -367,37 +371,35 @@
             cols = slice((s % 2) * BLK, (s % 2 + 1) * BLK)
             img_ref[rows, cols] = value
             high[rows, cols], low[rows, cols] = split(value)
-        for half in range(2):
-            top = half * BLK + sub * HALF
-            rows = slice(top, top + HALF)
-            halo_out[0, sub, half] = high[rows, PH - 128 : PH]
-            halo_out[1, sub, half] = high[rows, 0:128]
+        tops = [half * BLK + sub * HALF for half in range(2)]
+        for d, lane in enumerate((PH - 128, 0)):
+            slab = jnp.concatenate([high[top : top + HALF, lane : lane + 128] for top in tops], axis=0)
+            outermost = lax.dot_general(pick[d], slab, (((1,), (1,)), ((), ())), preferred_element_type=F32)
+            halo_out[d, sub] = outermost.astype(BF16)
         for d in range(2):
             halo_copy(d, sub).start()
 
     high[...], low[...] = split(dot3(high[...], low[...], col_tab[0], col_tab[1]))
-    for sub in range(2):
-        for d in range(2):
-            halo_copy(d, sub).wait_recv()
-    dot = lambda a, b: jnp.dot(a, b, preferred_element_type=F32)
-    sides = [jnp.concatenate([halo_in[d, n % 2, n // 2] for n in range(4)], axis=0) for d in range(2)]
-    left, right = sides
-    from_left = dot(left, col_tab[0, 0:128, 128:256]) + dot(left, col_tab[1, 0:128, 128:256])
-    from_right = dot(right, col_tab[0, 128:256, 0:128]) + dot(right, col_tab[1, 128:256, 0:128])
-    edge_high, edge_low = split(jnp.concatenate([from_left, from_right], axis=1))
     height = PH // NBAND
     part = height // 2
     opposite = lax.rem(band + 2, NBAND)
     near = (above, below)
     over_noise = (1.0 / jnp.full((8, 128), noise_ref[0], F32))[0:1, 0:1]
 
-    def rows_of(first, chunks):
-        row_high = jnp.concatenate([row_tab[0, g] for g in chunks], axis=0)
-        row_low = jnp.concatenate([row_tab[1, g] for g in chunks], axis=0)
-        row = dot3(row_high, row_low, high[...], low[...])
-        edge = dot3(row_high, row_low, edge_high, edge_low)
+    def row_tables(chunks):
+        return [jnp.concatenate([row_tab[n, g] for g in chunks], axis=0) for n in range(2)]
+
+    def rows_of(first, chunks, main=None):
+        tables = row_tables(chunks)
+        row = dot3(*tables, high[...], low[...]) if main is None else main
+        edge = dot3(*tables, edge_high, edge_low)
+        on_left = lax.broadcasted_iota(jnp.int32, edge.shape, 1) < 64
         row = jnp.concatenate(
-            [row[:, 0:128] + edge[:, 0:128], row[:, 128 : PH - 128], row[:, PH - 128 : PH] + edge[:, 128:256]],
+            [
+                row[:, 0:128] + jnp.where(on_left, edge, 0.0),
+                row[:, 128 : PH - 128],
+                row[:, PH - 128 : PH] + jnp.where(on_left, 0.0, edge),
+            ],
             axis=1,
         )
         squares = row * row * jnp.broadcast_to(over_noise, row.shape)
@@ -413,13 +415,30 @@
         near_out[d, 1 - d] = term[1 + d, (1 - d) * part : (2 - d) * part].astype(BF16)
         near_copy(d, 1 - d).start()
 
-    rows_of(0, (opposite, above))
+    main = dot3(*row_tables((opposite,)), high[...], low[...])
+    for sub in range(2):
+        for d in range(2):
+            halo_copy(d, sub).wait_recv()
+    dot = lambda a, b: jnp.dot(a, b, preferred_element_type=F32)
+    sides = [
+        jnp.concatenate([halo_in[d, n % 2, :, n // 2 * HALF : n // 2 * HALF + HALF] for n in range(4)], axis=1)
+        for d in range(2)
+    ]
+    gap = jnp.zeros((128 - EDGE, PH), BF16)
+    sides = jnp.concatenate([gap, *sides, gap], axis=0)
+    edge_turned = jnp.zeros((128, PH), F32)
+    for n in range(2):
+        corners = jnp.concatenate([row_tab[n, 1, :, 0:128], row_tab[n, 0, :, 128:256]], axis=1)
+        edge_turned = edge_turned + jnp.dot(corners, sides, preferred_element_type=F32)
+    edge_high, edge_low = split(edge_turned.T)
+    rows_of(0, (opposite,), main)
     for d in range(2):
         far_out[d] = term[0, d * part : (d + 1) * part].astype(BF16)
         far_copy(d).start()
+    rows_of(1, (above, below))
     send_early(0)
-    rows_of(2, (below, band))
     send_early(1)
+    rows_of(3, (band,))
     for d in range(2):
         far_copy(d).wait_recv()
         near_out[d, d] = (term[1 + d, d * part : (d + 1) * part] + far_in[d].astype(F32)).astype(BF16)
@@ -467,8 +486,8 @@
             pltpu.VMEM((2 * SIDE - 2, SIDE, 8, 128), F32),
             pltpu.VMEM((SIDE - 1, SIDE, 8, 128), F32),
             pltpu.VMEM((SIDE - 1, SIDE, 8, 128), F32),
-            pltpu.VMEM((2, 2, 2, HALF, 128), BF16),
-            pltpu.VMEM((2, 2, 2, HALF, 128), BF16),
+            pltpu.VMEM((2, 2, EDGE, BLK), BF16),
+            pltpu.VMEM((2, 2, EDGE, BLK), BF16),
             pltpu.VMEM((2, PH, PH), BF16),
             pltpu.VMEM((2, PH // 128, 128, PH), BF16),
             pltpu.VMEM((PH, PH), BF16),

time: 77.1 us -> 76.3 us (0.990)
  Pallas kernels: 75.7 us -> 74.8 us
    pallas_call x1, Pallas kernels: 68.1 us -> 67.2 us  [reduce_partials(): pl.pallas_call(reduce_kernel, out_shape=(jax.ShapeDtypeStruct((PH, PH), F...]
where the time goes in v6:
time: 76.3 us; the launch traced here: 76.1 us
  Pallas kernels  74.8 us (98%)
  between operations  1.32 us (2%)
    pallas_call x1, Pallas kernels, reduce_partials(): pl.pallas_call(reduce_kernel, out_shape=(jax.ShapeDtypeStruct((PH, PH), F...  67.2 us
    pallas_call x1, Pallas kernels, match_partials(): pl.pallas_call(match_kernel, out_shape=pltpu.VMEM((NPATCH * SLOTS + 1, BL...  6.53 us

profile of v6, /device:TPU:0, one launch (start us, length us, event | category | flops | bytes accessed | tf_op | source)
XLA Modules:
  0.0 76.1 jit_solution(2367632456309448649)
XLA Ops:
  0.6 0.0 copy-start
  1.3 6.5 %match_partials.1.d_ref = bf16[129,256,256]{2,1,0:T(8,128)(2,1)S(1)} custom-call(s32[1,32]{1,0:T(1,128)} %patch_hbm.1, s32[1,32]{1,0:T(1,128)} %slot_hbm.1, bf16[1,32]{1,0:T(2,128)(2,1)} %weight_hbm.1, bf16[1,32,2,41]{3,2,1,0:T(2,128)(2,1)} %taps_hbm.1, bf16[1,32,256,256]{3,2,1,0:T(8,128)(2,1)} %blocks_hbm.1), custom_call_target="tpu_custom_call" | custom-call | tf_op jit(solution)/shard_map/match_partials/pallas_call | solution.py:120
  7.8 0.0 copy-done
  7.9 67.2 %reduce_partials.1 = (f32[512,512]{1,0:T(8,128)S(1)}, f32[128,512]{1,0:T(8,128)S(1)}) custom-call(bf16[129,256,256]{2,1,0:T(8,128)(2,1)S(1)} %match_partials.1.d_ref, f32[25]{0:T(128)S(1)} %bitcast.2, f32[1]{0:T(128)S(6)} %copy.9.noise_ref), custom_call_target="tpu_custom_call" | custom-call | tf_op jit(solution)/shard_map/reduce_partials/pallas_call | solution.py:472
  75.1 1.1 %write_out.1 = (f32[512,512]{1,0:T(8,128)}, f32[128,512]{1,0:T(8,128)}) custom-call(f32[512,512]{1,0:T(8,128)S(1)} %get-tuple-element.6.image, f32[128,512]{1,0:T(8,128)S(1)} %get-tuple-element.7.chi), custom_call_target="tpu_custom_call" | custom-call | tf_op jit(solution)/shard_map/write_out/pallas_call | solution.py:530
Async XLA Ops:
  0.6 7.2 %copy-start = (f32[1,25]{1,0:T(1,128)S(1)}, f32[1,25]{1,0:T(1,128)}, u32[]{:S(2)}) copy-start(f32[1,25]{1,0:T(1,128)} %param.12) | copy-start | bytes 304

commit v7 on v6

--- a/solution.py
+++ b/solution.py
@@ -164,7 +164,7 @@
     offset = sign * offset + shift + DR
     block = jnp.zeros((128, 128), F32)
     for t in range(DTAPS):
-        block = jnp.where(offset == t, det_ref[t], block)
+        block = jnp.where(offset == t, det_ref[0, t], block)
     return block
 
 
@@ -185,11 +185,13 @@
 
 
 def reduce_kernel(
-    d_ref, det_ref, noise_ref, img_ref, chi_ref,
-    pair, hop1, hop2, w_ref, w_pair, w_acc, w_hop1, w_hop2, halo_out, halo_in, col_tab, row_tab, high, low,
+    d_ref, det_hbm, noise_ref, img_ref, chi_ref,
+    det_ref,    pair, hop1, hop2, w_ref, w_pair, w_acc, w_hop1, w_hop2, halo_out, halo_in, col_tab, row_tab, high, low,
     term, far_out, far_in, near_out, near_in,
-    pair_sem, hop1_sem, hop2_sem, send_sem, w_sem, halo_sem, far_sem, near_sem, end_sem,
+    pair_sem, hop1_sem, hop2_sem, send_sem, w_sem, halo_sem, far_sem, near_sem, end_sem, small_sem,
 ):
+    taps_copy = pltpu.make_async_copy(det_hbm, det_ref, small_sem.at[0])
+    taps_copy.start()
     me = lax.axis_index("patch")
     band = lax.axis_index("band")
     core = lax.rem(me, 2)
@@ -336,6 +338,7 @@
 
     w_step(0)
     start_units(0, (1, 0))
+    taps_copy.wait()
     build_tables(det_ref, col_tab, row_tab)
     pass_units(1, 0, (2, 0))
     w_step(1)
@@ -384,7 +387,7 @@
     part = height // 2
     opposite = lax.rem(band + 2, NBAND)
     near = (above, below)
-    over_noise = (1.0 / jnp.full((8, 128), noise_ref[0], F32))[0:1, 0:1]
+    over_noise = 1.0 / noise_ref[...]
 
     def row_tables(chunks):
         return [jnp.concatenate([row_tab[n, g] for g in chunks], axis=0) for n in range(2)]
@@ -465,7 +468,8 @@
 
 
 def reduce_partials(partial, det_taps, noise_var):
-    smem = pl.BlockSpec(memory_space=pltpu.SMEM)
+    hbm = pl.BlockSpec(memory_space=pltpu.HBM)
+    keep = lambda x: pltpu.with_memory_space_constraint(x, pltpu.HBM)
     vmem = pl.BlockSpec(memory_space=pltpu.VMEM)
     dma = pltpu.SemaphoreType.DMA
     height = PH // NBAND
@@ -475,9 +479,10 @@
             jax.ShapeDtypeStruct((PH, PH), F32),
             jax.ShapeDtypeStruct((height, PH), F32),
         ),
-        in_specs=[vmem, smem, smem],
+        in_specs=[vmem, hbm, vmem],
         out_specs=(vmem, vmem),
         scratch_shapes=[
+            pltpu.SMEM(det_taps.shape, F32),
             pltpu.VMEM((SLOTS, SIDE, SIDE, BLK, BLK), BF16),
             pltpu.VMEM((SLOTS, SIDE - 1, SIDE, BLK, BLK), BF16),
             pltpu.VMEM((SLOTS, SIDE - 1, BLK, BLK), BF16),
@@ -506,12 +511,13 @@
             dma((2,)),
             dma((4,)),
             dma((10,)),
+            dma((1,)),
         ],
         compiler_params=pltpu.CompilerParams(
             vmem_limit_bytes=36 << 20, collective_id=0, has_side_effects=True
         ),
         name="reduce_partials",
-    )(partial, det_taps, noise_var)
+    )(partial, keep(det_taps), noise_var)
 
 
 def write_kernel(image, chi, image_hbm, chi_hbm, sems):
@@ -540,7 +546,7 @@
 def local(blocks, dest_patch, dest_slot, weights, psf_taps, det_taps, noise_var):
     partial = match_partials(blocks, dest_patch, dest_slot, weights, psf_taps)
     partial = pltpu.with_memory_space_constraint(partial, pltpu.VMEM)
-    image, chi = reduce_partials(partial, det_taps[0], noise_var)
+    image, chi = reduce_partials(partial, det_taps, noise_var.reshape(1, 1))
     image, chi = write_out(image, chi)
     return image[None], chi
 

time: 76.3 us -> 75.7 us (level)
  no operation moved by 1% of the time
where the time goes in v7:
time: 75.7 us; the launch traced here: 75.6 us
  Pallas kernels  74.3 us (98%)
  between operations  1.29 us (2%)
    pallas_call x1, Pallas kernels, reduce_partials(): pl.pallas_call(reduce_kernel, out_shape=(jax.ShapeDtypeStruct((PH, PH), F...  66.7 us
    pallas_call x1, Pallas kernels, match_partials(): pl.pallas_call(match_kernel, out_shape=pltpu.VMEM((NPATCH * SLOTS + 1, BL...  6.53 us

profile of v7, /device:TPU:0, one launch (start us, length us, event | category | flops | bytes accessed | tf_op | source)
XLA Modules:
  0.0 75.6 jit_solution(13056923579398401479)
XLA Ops:
  1.3 6.5 %match_partials.1.d_ref = bf16[129,256,256]{2,1,0:T(8,128)(2,1)S(1)} custom-call(s32[1,32]{1,0:T(1,128)} %patch_hbm.1, s32[1,32]{1,0:T(1,128)} %slot_hbm.1, bf16[1,32]{1,0:T(2,128)(2,1)} %weight_hbm.1, bf16[1,32,2,41]{3,2,1,0:T(2,128)(2,1)} %taps_hbm.1, bf16[1,32,256,256]{3,2,1,0:T(8,128)(2,1)} %blocks_hbm.1), custom_call_target="tpu_custom_call" | custom-call | tf_op jit(solution)/shard_map/match_partials/pallas_call | solution.py:120
  7.8 66.7 %reduce_partials.1 = (f32[512,512]{1,0:T(8,128)S(1)}, f32[128,512]{1,0:T(8,128)S(1)}) custom-call(bf16[129,256,256]{2,1,0:T(8,128)(2,1)S(1)} %match_partials.1.d_ref, f32[1,25]{1,0:T(1,128)} %det_hbm.1, f32[1,1]{1,0:T(1,128)} %bitcast.2.noise_ref), custom_call_target="tpu_custom_call" | custom-call | tf_op jit(solution)/shard_map/reduce_partials/pallas_call | solution.py:476
  74.5 1.1 %write_out.1 = (f32[512,512]{1,0:T(8,128)}, f32[128,512]{1,0:T(8,128)}) custom-call(f32[512,512]{1,0:T(8,128)S(1)} %get-tuple-element.6.image, f32[128,512]{1,0:T(8,128)S(1)} %get-tuple-element.7.chi), custom_call_target="tpu_custom_call" | custom-call | tf_op jit(solution)/shard_map/write_out/pallas_call | solution.py:536

commit v8 on v7

--- a/solution.py
+++ b/solution.py
@@ -54,9 +54,11 @@
             ((taps_hbm, taps_ref), (weight_hbm, weight_ref), (patch_hbm, patch_ref), (slot_hbm, slot_ref))
         )
     ]
-    for copy in small:
+    small[0].start()
+    fetch(0).start()
+    for copy in small[1:]:
         copy.start()
-    for g in range(count // GROUP):
+    for g in range(1, count // GROUP):
         fetch(g).start()
     even_mats[...] = jnp.zeros_like(even_mats)
     odd_mats[...] = jnp.zeros_like(odd_mats)
@@ -521,9 +523,9 @@
 
 
 def write_kernel(image, chi, image_hbm, chi_hbm, sems):
-    copies = [
-        pltpu.make_async_copy(src, dst, sems.at[n]) for n, (src, dst) in enumerate(((image, image_hbm), (chi, chi_hbm)))
-    ]
+    parts = [pl.ds(n * HALF, HALF) for n in range(PH // HALF)]
+    copies = [pltpu.make_async_copy(image.at[rows], image_hbm.at[rows], sems.at[n]) for n, rows in enumerate(parts)]
+    copies.append(pltpu.make_async_copy(chi, chi_hbm, sems.at[len(parts)]))
     for copy in copies:
         copy.start()
     for copy in copies:
@@ -538,7 +540,7 @@
         out_shape=tuple(jax.ShapeDtypeStruct(x.shape, x.dtype) for x in (image, chi)),
         in_specs=[vmem, vmem],
         out_specs=(hbm, hbm),
-        scratch_shapes=[pltpu.SemaphoreType.DMA((2,))],
+        scratch_shapes=[pltpu.SemaphoreType.DMA((PH // HALF + 1,))],
         name="write_out",
     )(*(pltpu.with_memory_space_constraint(x, pltpu.VMEM) for x in (image, chi)))
 

time: 75.7 us -> 75.7 us (level)
  no operation moved by 1% of the time
where the time goes in v8:
time: 75.7 us; the launch traced here: 75.6 us
  Pallas kernels  74.3 us (98%)
  between operations  1.29 us (2%)
    pallas_call x1, Pallas kernels, reduce_partials(): pl.pallas_call(reduce_kernel, out_shape=(jax.ShapeDtypeStruct((PH, PH), F...  66.7 us
    pallas_call x1, Pallas kernels, match_partials(): pl.pallas_call(match_kernel, out_shape=pltpu.VMEM((NPATCH * SLOTS + 1, BL...  6.53 us

profile of v8, /device:TPU:0, one launch (start us, length us, event | category | flops | bytes accessed | tf_op | source)
XLA Modules:
  0.0 75.6 jit_solution(8770148707204553552)
XLA Ops:
  1.3 6.5 %match_partials.1.d_ref = bf16[129,256,256]{2,1,0:T(8,128)(2,1)S(1)} custom-call(s32[1,32]{1,0:T(1,128)} %patch_hbm.1, s32[1,32]{1,0:T(1,128)} %slot_hbm.1, bf16[1,32]{1,0:T(2,128)(2,1)} %weight_hbm.1, bf16[1,32,2,41]{3,2,1,0:T(2,128)(2,1)} %taps_hbm.1, bf16[1,32,256,256]{3,2,1,0:T(8,128)(2,1)} %blocks_hbm.1), custom_call_target="tpu_custom_call" | custom-call | tf_op jit(solution)/shard_map/match_partials/pallas_call | solution.py:122
  7.8 66.7 %reduce_partials.1 = (f32[512,512]{1,0:T(8,128)S(1)}, f32[128,512]{1,0:T(8,128)S(1)}) custom-call(bf16[129,256,256]{2,1,0:T(8,128)(2,1)S(1)} %match_partials.1.d_ref, f32[1,25]{1,0:T(1,128)} %det_hbm.1, f32[1,1]{1,0:T(1,128)} %bitcast.2.noise_ref), custom_call_target="tpu_custom_call" | custom-call | tf_op jit(solution)/shard_map/reduce_partials/pallas_call | solution.py:478
  74.5 1.1 %write_out.1 = (f32[512,512]{1,0:T(8,128)}, f32[128,512]{1,0:T(8,128)}) custom-call(f32[512,512]{1,0:T(8,128)S(1)} %get-tuple-element.6.image, f32[128,512]{1,0:T(8,128)S(1)} %get-tuple-element.7.chi), custom_call_target="tpu_custom_call" | custom-call | tf_op jit(solution)/shard_map/write_out/pallas_call | solution.py:538
